TPU v7x, 256 devices: a whole 4x4x8 slice. The times are simulated.
256 devices in a mesh: dom: 64 (over x, z, core), rep: 4 (over y).
Axes of the slice: x: 4, y: 4, z: 8, core: 2. Of those that a mesh axis runs over, the one named last changes fastest.
Arguments:
- spline_blocks: bfloat16 [2048, 2, 64, 128], P(('dom', 'rep')), may hold values from -0.75 to 0.75
- modal_coeff: bfloat16 [64, 2, 8], replicated, may hold values from -6 to 6
- frequency: float32 [8], replicated, may hold values from 0.2 to 0.8
- face_dest: int32 [262144, 1], P('dom'), may hold values from 0 to 63; in each aligned block of 4096 rows (0 to 4095, 4096 to 8191, ...) at most 128 rows name the same one
- face_cell: int32 [262144], P('dom'), may hold values from 0 to 2047
- wall_weight: float32 [5, 2, 131072], P(None, None, 'dom'), may hold values from -6 to 6
- flow_rhs: float32 [5, 2, 8, 131072], P(None, None, 'rep', 'dom'), may hold values from -6 to 6
- previous: float32 [5, 2, 8, 131072], P(None, None, 'rep', 'dom'), may hold values from -6 to 6
- diag_inverse: float32 [5, 5, 131072], P(None, None, 'dom'), may hold values from -0.3 to 1.2
- off_jacobian: bfloat16 [6, 5, 5, 131072], P(None, None, None, 'dom'), may hold values from -0.5 to 0.5
- neighbor: int32 [6, 131072], P(None, 'dom'), may hold values from 0 to 3071, as said below
- send_list: int32 [4, 16384], P(None, 'dom'), may hold values from 0 to 2047
Outputs:
- solution: float32 [5, 2, 8, 131072], P(None, None, 'rep', 'dom')
Inputs may be any that keep to these rules, and one draw needn't show every extreme that they name: `face_dest`: in each aligned block of 4096 rows (the rows of one index of dom), no partition is named by more than 128 rows, and in every draw some partition is named by exactly 128 rows of some block. `neighbor`: entries below 2048 name a cell of the same partition; entry 2048 + k * 256 + i names ghost row i of block k.
All inputs are finite; a program needn't handle non-finite values.
Results may differ from a plain program's by a relative error of at most 0.0003.
Values may be sent and summed in bfloat16 or wider, within the bound.
No kernel may reach another device: no remote copies, remote signals or barrier semaphores. Data moves between devices by JAX's collectives and lax.ppermute only.
A program may use at most 64 MiB of HBM per device.

v0:
```python
import jax
import jax.numpy as jnp
from jax import lax
from jax.sharding import PartitionSpec as P

SWEEPS = 2


def from_behind(value, axis, by):
    length = lax.axis_size(axis)
    return lax.ppermute(value, axis, [(i, (i + by) % length) for i in range(length)])


def face_values(blocks_in, coeff_in, freq_in):
    mode_count = coeff_in.shape[0]
    column_count = coeff_in.shape[2]
    flat_coeff = coeff_in.reshape(mode_count, 2 * column_count)
    products = jnp.einsum(
        "kqmr,mz->qzkr", blocks_in, flat_coeff, preferred_element_type=jnp.float32
    )
    products = products.reshape(2, 2, column_count, blocks_in.shape[0] * blocks_in.shape[3])
    angular = freq_in[:, None]
    velocity = jnp.stack([-angular * products[0, 1], angular * products[0, 0]])
    return jnp.stack([velocity, products[1]])


def shards(
    spline_blocks,
    modal_coeff,
    frequency,
    face_dest,
    face_cell,
    wall_weight,
    flow_rhs,
    previous,
    diag_inverse,
    off_jacobian,
    neighbor,
    send_list,
):
    pair_dev = flow_rhs.shape[2]
    cell_count = flow_rhs.shape[3]
    dom_size = lax.axis_size("dom")
    first_pair = lax.axis_index("rep") * pair_dev
    own_freq = lax.dynamic_slice_in_dim(frequency, first_pair, pair_dev, 0)
    own_coeff = lax.dynamic_slice_in_dim(modal_coeff, first_pair, pair_dev, 2)
    face_data = face_values(
        lax.all_gather(spline_blocks, "rep", axis=0, tiled=True), own_coeff, own_freq
    )
    row_count = face_data.shape[3]
    capacity = 2 * row_count // dom_size
    destination = face_dest[:, 0]
    one_hot = (destination[:, None] == jnp.arange(dom_size, dtype=jnp.int32)[None, :]).astype(
        jnp.int32
    )
    position = jnp.sum(jnp.cumsum(one_hot, axis=0) * one_hot, axis=1) - 1
    slot_flat = destination * capacity + position
    values = face_data.reshape(4 * pair_dev, row_count)
    send_values = (
        jnp.zeros((4 * pair_dev, dom_size * capacity), jnp.float32).at[:, slot_flat].set(values)
    )
    send_cells = (
        jnp.full((1, dom_size * capacity), cell_count, jnp.float32)
        .at[0, slot_flat]
        .set(face_cell.astype(jnp.float32))
    )
    recv_values, recv_cells = (
        lax.all_to_all(
            send_values.reshape(4 * pair_dev, dom_size, capacity),
            "dom",
            split_axis=1,
            concat_axis=1,
            tiled=True,
        ),
        lax.all_to_all(
            send_cells.reshape(1, dom_size, capacity),
            "dom",
            split_axis=1,
            concat_axis=1,
            tiled=True,
        ),
    )
    cell_target = recv_cells.reshape(-1).astype(jnp.int32)
    wall_sum = (
        jnp.zeros((4 * pair_dev, cell_count), jnp.float32)
        .at[:, cell_target]
        .add(recv_values.reshape(4 * pair_dev, -1), mode="drop")
    )
    wall_sum = wall_sum.reshape(2, 2 * pair_dev, cell_count)
    row_width = 2 * pair_dev
    rhs_full = (
        flow_rhs.reshape(5, row_width, cell_count)
        + wall_weight[:, 0, None, :] * wall_sum[0][None]
        + wall_weight[:, 1, None, :] * wall_sum[1][None]
    )
    halo_count = send_list.shape[1]
    jac_faces = jnp.transpose(off_jacobian, (1, 2, 0, 3))
    neighbor_flat = neighbor.reshape(-1)
    angular = own_freq[None, :, None]
    iterate = previous
    for sweep_index in range(SWEEPS):
        flat_field = iterate.reshape(5 * row_width, cell_count)
        picked = jnp.take(flat_field, send_list.reshape(-1), axis=1)
        from_below = from_behind(picked[:, 0:halo_count], "dom", 1)
        from_above = from_behind(picked[:, halo_count : 2 * halo_count], "dom", -1)
        far_below = from_behind(picked[:, 2 * halo_count : 3 * halo_count], "dom", 2)
        far_above = from_behind(picked[:, 3 * halo_count :], "dom", -2)
        extended = jnp.concatenate(
            [flat_field, from_below, from_above, far_below, far_above], axis=1
        )
        beside = jnp.take(extended, neighbor_flat, axis=1).reshape(5, row_width, 6, cell_count)
        coupling = jnp.sum(
            jac_faces[:, :, None, :, :].astype(jnp.float32) * beside[None], axis=(1, 3)
        )
        spinning = jnp.stack([-angular * iterate[:, 1], angular * iterate[:, 0]], axis=1).reshape(
            5, row_width, cell_count
        )
        residual_now = rhs_full - coupling - spinning
        update = jnp.sum(diag_inverse[:, :, None, :] * residual_now[None], axis=1)
        iterate = update.reshape(5, 2, pair_dev, cell_count)
    return iterate


def solution(mesh):
    return jax.shard_map(
        shards,
        mesh=mesh,
        in_specs=(
            P(("dom", "rep"), None, None, None),
            P(),
            P(),
            P("dom", None),
            P("dom"),
            P(None, None, "dom"),
            P(None, None, "rep", "dom"),
            P(None, None, "rep", "dom"),
            P(None, None, "dom"),
            P(None, None, None, "dom"),
            P(None, "dom"),
            P(None, "dom"),
        ),
        out_specs=P(None, None, "rep", "dom"),
        check_vma=False,
    )
```

profile of v0, /device:TPU:8, one launch (start us, length us, event | category | flops | bytes accessed | tf_op | source)
XLA Modules:
  0.0 336.8 jit_solution(17069681349740002035)
XLA Ops:
  6.5 0.7 copy.112
  7.3 1.0 reshape.205
  8.3 0.4 copy.100
  8.7 2.8 gather_fusion
  11.5 0.2 select_bitcast_fusion.3
  11.7 0.8 fusion.17
  12.5 7.5 %collective-permute-start.1 = (f32[20,256]{0,1:T(8,128)}, f32[20,256]{0,1:T(8,128)}, u32[]{:S(2)}, u32[]{:S(2)}) collective-permute-start(f32[20,256]{0,1:T(8,128)} %get-tuple-element.17), channel_id=1, source_target_pairs={{0,252},{4,0},{8,4},{12,8},{16,12},{20,16},{24,20},{28,24},{32,28}... | collective-permute-start | bytes 61448 | tf_op jit(solution)/shard_map/ppermute | solution.py:11
  20.0 5.3 %collective-permute-start.3 = (f32[20,256]{0,1:T(8,128)}, f32[20,256]{0,1:T(8,128)}, u32[]{:S(2)}, u32[]{:S(2)}) collective-permute-start(f32[20,256]{0,1:T(8,128)} %get-tuple-element.15), channel_id=1, source_target_pairs={{0,248},{4,252},{8,0},{12,4},{16,8},{20,12},{24,16},{28,20},{32,24... | collective-permute-start | bytes 61448 | tf_op jit(solution)/shard_map/ppermute | solution.py:11
  25.5 18.4 %reduce-window.6 = s32[64,32,128]{2,1,0:T(8,128)S(1)} reduce-window(s32[64,32,128]{2,1,0:T(8,128)S(1)} %fusion.4, s32[]{:T(128)} %constant.11.clone.1), window={size=1x1x128 pad=0_0x0_0x127_0}, to_apply=%region_0.0 | reduce-window | flops 33292288 | bytes 2097156 | tf_op jit(solution)/shard_map/reduce-window
  43.9 0.3 slice.98
  44.3 0.4 copy.108
  45.0 0.3 broadcast_add_fusion
  45.3 0.8 fusion.3
  46.5 16.1 %scatter_custom_fusion.2 = f32[8192]{0:T(1024)} fusion(s32[4096]{0:T(1024)S(1)} %broadcast_select_fusion, f32[4096]{0:T(1024)S(1)} %convert_element_type.30, f32[]{:T(128)} %constant.9.clone.1), kind=kCustom, calls=%fused_computation.63 | custom fusion | bytes 32772
  62.6 5.6 %all-to-all-start = ((f32[1,64,128]{2,0,1:T(1,128)}), f32[1,64,128]{2,0,1:T(1,128)}, u32[]{:S(2)}, u32[]{:S(2)}) async-start(f32[1,64,128]{2,0,1:T(1,128)} %bitcast.7), calls=%async_computation | async-start | bytes 65536 | tf_op jit(solution)/shard_map/all_to_all | solution.py:75
  68.2 0.2 all-gather.2.cloned.1.call-start
  68.4 0.5 all-gather.2.cloned.1.call-update
  69.0 0.6 fusion.7
  69.7 1.3 convert_bitcast_fusion
  71.1 0.7 fusion.14
  72.0 0.7 copy_bitcast_fusion
  72.7 0.5 constant_dynamic-slice_fusion
  73.4 1.1 reshape.197
  74.5 0.9 constant_dynamic-update-slice_fusion.3
  75.4 0.9 constant_dynamic-update-slice_fusion.2
  76.3 0.9 constant_dynamic-update-slice_fusion.1
  77.3 0.9 constant_dynamic-update-slice_fusion
  78.2 45.0 %gather_fusion.1 = f32[12288,20]{1,0:T(8,128)} fusion(f32[20,3072]{0,1:T(8,128)S(1)} %constant_dynamic-update-slice_fusion, s32[12288]{0:T(1024)} %fusion.7), kind=kCustom, calls=%fused_computation.1.clone | custom fusion | bytes 2015232 | tf_op jit(solution)/shard_map/jit(_take)/gather | solution.py:111
  123.2 10.4 %select_bitcast_fusion.1 = f32[20,12288]{0,1:T(8,128)} fusion(f32[12288,20]{1,0:T(8,128)} %gather_fusion.1, pred[12288]{0:T(1024)(128)(4,1)S(1)} %compare_and_fusion), kind=kLoop, calls=%fused_computation.8 | loop fusion | flops 245760 | bytes 1978368 | tf_op jit(solution)/shard_map/jit(_take)/select_n | solution.py:111
  133.6 5.5 %copy.101 = f32[20,12288]{1,0:T(8,128)} copy(f32[20,12288]{0,1:T(8,128)} %select_bitcast_fusion.1) | data formatting | bytes 1966080 | tf_op jit(solution)/shard_map/jit(_take)/select_n | solution.py:111
  139.1 1.8 mul.189
  140.9 0.6 copy.102
  141.5 1.7 multiply_reduce_fusion.1
  143.2 1.5 convolution_bitcast_fusion
  145.2 2.0 copy.93
  147.2 13.1 %scatter_custom_fusion = f32[8,8192]{0,1:T(8,128)} fusion(s32[4096]{0:T(1024)} %bitcast.74, f32[4096,8]{1,0:T(8,128)} %copy.93, f32[]{:T(128)} %constant.8.clone.1), kind=kCustom, calls=%fused_computation.11 | custom fusion | bytes 262656 | tf_op jit(solution)/shard_map/scatter | solution.py:60
  160.3 3.5 %copy.94 = f32[8,64,128]{2,0,1:T(8,128)} copy(f32[8,64,128]{0,2,1:T(8,128)} %bitcast.67) | data formatting | bytes 524288 | tf_op jit(solution)/shard_map/reshape | solution.py:69
  163.7 10.2 %all-to-all-start.1 = ((f32[8,64,128]{2,0,1:T(8,128)}), f32[8,64,128]{2,0,1:T(8,128)S(1)}, u32[]{:S(2)}, u32[]{:S(2)}) async-start(f32[8,64,128]{2,0,1:T(8,128)} %copy.94), calls=%async_computation.1 | async-start | bytes 524288 | tf_op jit(solution)/shard_map/all_to_all | solution.py:68
  174.0 0.8 compare_select_fusion
  174.8 11.2 %all-to-all-done.1 = f32[8,64,128]{2,0,1:T(8,128)S(1)} async-done(((f32[8,64,128]{2,0,1:T(8,128)}), f32[8,64,128]{2,0,1:T(8,128)S(1)}, u32[]{:S(2)}, u32[]{:S(2)}) %all-to-all-start.1) | async-done | bytes 262176 | tf_op jit(solution)/shard_map/all_to_all | solution.py:68
  186.0 2.6 copy.95
  188.6 44.8 %scatter_custom_fusion.1 = f32[8,2048]{0,1:T(8,128)S(1)} fusion(s32[8192]{0:T(1024)S(1)} %bitcast.80, f32[8192,8]{1,0:T(8,128)} %copy.95, f32[]{:T(128)} %constant.8.clone.1), kind=kCustom, calls=%fused_computation.26 | custom fusion | flops 65536 | bytes 66048 | tf_op jit(solution)/shard_map/scatter-add | solution.py:87
  233.4 1.7 fusion.15
  235.0 1.7 copy.98
  236.7 0.9 copy.96
  237.6 1.1 subtract_subtract_fusion.1
  239.2 1.3 copy.104
  240.5 1.3 constant_dynamic-update-slice_fusion.9
  241.8 5.2 %gather_fusion.2 = f32[1024,20]{1,0:T(8,128)} fusion(f32[20,2048]{0,1:T(8,128)} %copy.104, s32[1024]{0:T(1024)S(1)} %copy-done.19), kind=kCustom, calls=%fused_computation.2.clone | custom fusion | bytes 167936 | tf_op jit(solution)/shard_map/jit(_take)/gather | solution.py:103
  247.0 0.7 slice_multiply_fusion.1
  247.8 1.2 select_bitcast_fusion.2
  249.0 0.8 fusion.16
  250.0 0.8 reshape.210
  250.8 5.0 %collective-permute-start.5 = (f32[20,256]{0,1:T(8,128)}, f32[20,256]{0,1:T(8,128)S(1)}, u32[]{:S(2)}, u32[]{:S(2)}) collective-permute-start(f32[20,256]{0,1:T(8,128)} %get-tuple-element.13), channel_id=1, source_target_pairs={{0,252},{4,0},{8,4},{12,8},{16,12},{20,16},{24,20},{28,24},{32,28}... | collective-permute-start | bytes 61448 | tf_op jit(solution)/shard_map/ppermute | solution.py:11
  255.8 5.3 %collective-permute-start.7 = (f32[20,256]{0,1:T(8,128)}, f32[20,256]{0,1:T(8,128)S(1)}, u32[]{:S(2)}, u32[]{:S(2)}) collective-permute-start(f32[20,256]{0,1:T(8,128)} %get-tuple-element.11), channel_id=1, source_target_pairs={{0,248},{4,252},{8,0},{12,4},{16,8},{20,12},{24,16},{28,20},{32,24... | collective-permute-start | bytes 61448 | tf_op jit(solution)/shard_map/ppermute | solution.py:11
  261.1 0.9 constant_dynamic-update-slice_fusion.8
  262.1 2.2 collective-permute-done.6
  264.3 45.0 %gather_fusion.3 = f32[12288,20]{1,0:T(8,128)} fusion(f32[20,3072]{0,1:T(8,128)S(1)} %constant_dynamic-update-slice_fusion.5, s32[12288]{0:T(1024)} %fusion.7), kind=kCustom, calls=%fused_computation.3.clone | custom fusion | bytes 2015232 | tf_op jit(solution)/shard_map/jit(_take)/gather | solution.py:111
  309.4 10.4 %select_bitcast_fusion = f32[20,12288]{0,1:T(8,128)} fusion(f32[12288,20]{1,0:T(8,128)} %gather_fusion.3, pred[12288]{0:T(1024)(128)(4,1)S(1)} %compare_and_fusion), kind=kLoop, calls=%fused_computation.7 | loop fusion | flops 245760 | bytes 1978368 | tf_op jit(solution)/shard_map/jit(_take)/select_n | solution.py:111
  319.7 5.5 %copy.105 = f32[20,12288]{1,0:T(8,128)} copy(f32[20,12288]{0,1:T(8,128)} %select_bitcast_fusion) | data formatting | bytes 1966080 | tf_op jit(solution)/shard_map/jit(_take)/select_n | solution.py:111
  325.2 1.8 mul.198
  327.0 0.6 copy.106
  327.7 1.1 multiply_reduce_fusion
  329.1 0.8 reshape.211
  (106 shorter events, 2.6 us)
Async XLA Ops:
  6.5 66.2 %copy-start = (bf16[64,2,8]{0,2,1:T(8,128)(2,1)S(1)}, bf16[64,2,8]{0,2,1:T(8,128)(2,1)}, u32[]{:S(2)}) copy-start(bf16[64,2,8]{0,2,1:T(8,128)(2,1)} %param.17) | copy-start | bytes 6148
  7.2 4.5 %copy-start.18 = (s32[1024]{0:T(1024)}, s32[1024]{0:T(1024)S(1)}, u32[]{:S(2)}) copy-start(s32[1024]{0:T(1024)S(1)} %fusion.13) | copy-start | bytes 12292
  7.3 4.5 %copy-start.21 = (pred[1024]{0:T(1024)(128)(4,1)}, pred[1024]{0:T(1024)(128)(4,1)S(1)}, u32[]{:S(2)}) copy-start(pred[1024]{0:T(1024)(128)(4,1)S(1)} %compare_and_fusion.1) | copy-start | bytes 3076
  8.7 16.7 %copy-start.2 = (f32[20,2048]{0,1:T(8,128)}, f32[20,2048]{0,1:T(8,128)S(1)}, u32[]{:S(2)}) copy-start(f32[20,2048]{0,1:T(8,128)S(1)} %copy.100) | copy-start | bytes 491524
  8.7 16.7 %copy-start.14 = (s32[4096,1]{0,1:T(1,128)S(1)}, s32[4096,1]{0,1:T(1,128)}, u32[]{:S(2)}) copy-start(s32[4096,1]{0,1:T(1,128)} %param.19) | copy-start | bytes 49156
  12.5 61.9 %collective-permute-start = (f32[20,256]{0,1:T(8,128)}, f32[20,256]{0,1:T(8,128)}, u32[]{:S(2)}, u32[]{:S(2)}) collective-permute-start(f32[20,256]{0,1:T(8,128)} %get-tuple-element.18), channel_id=1, source_target_pairs={{0,4},{4,8},{8,12},{12,16},{16,20},{20,24},{24,28},{28,32},{32,36}... | collective-permute-start | bytes 61448 | tf_op jit(solution)/shard_map/ppermute | solution.py:11
  12.5 62.9 %collective-permute-start.1 = (f32[20,256]{0,1:T(8,128)}, f32[20,256]{0,1:T(8,128)}, u32[]{:S(2)}, u32[]{:S(2)}) collective-permute-start(f32[20,256]{0,1:T(8,128)} %get-tuple-element.17), channel_id=1, source_target_pairs={{0,252},{4,0},{8,4},{12,8},{16,12},{20,16},{24,20},{28,24},{32,28}... | collective-permute-start | bytes 61448 | tf_op jit(solution)/shard_map/ppermute | solution.py:11
  20.0 56.3 %collective-permute-start.2 = (f32[20,256]{0,1:T(8,128)}, f32[20,256]{0,1:T(8,128)}, u32[]{:S(2)}, u32[]{:S(2)}) collective-permute-start(f32[20,256]{0,1:T(8,128)} %get-tuple-element.16), channel_id=1, source_target_pairs={{0,8},{4,12},{8,16},{12,20},{16,24},{20,28},{24,32},{28,36},{32,40... | collective-permute-start | bytes 61448 | tf_op jit(solution)/shard_map/ppermute | solution.py:11
  20.0 57.2 %collective-permute-start.3 = (f32[20,256]{0,1:T(8,128)}, f32[20,256]{0,1:T(8,128)}, u32[]{:S(2)}, u32[]{:S(2)}) collective-permute-start(f32[20,256]{0,1:T(8,128)} %get-tuple-element.15), channel_id=1, source_target_pairs={{0,248},{4,252},{8,0},{12,4},{16,8},{20,12},{24,16},{28,20},{32,24... | collective-permute-start | bytes 61448 | tf_op jit(solution)/shard_map/ppermute | solution.py:11
  44.9 1.3 copy-start.28
  44.9 1.4 copy-start.27
  45.0 1.5 copy-start.20
  45.3 23.6 %copy-start.3 = (f32[20,2048]{0,1:T(8,128)S(1)}, f32[20,2048]{0,1:T(8,128)}, u32[]{:S(2)}) copy-start(f32[20,2048]{0,1:T(8,128)} %copy-done.2) | copy-start | bytes 491524
  46.1 22.9 %copy-start.17 = (s32[6,2048]{1,0:T(8,128)S(1)}, s32[6,2048]{1,0:T(8,128)}, u32[]{:S(2)}) copy-start(s32[6,2048]{1,0:T(8,128)} %param.26) | copy-start | bytes 147460
  46.2 23.5 %copy-start.15 = (s32[4096,1]{0,1:T(1,128)}, s32[4096,1]{0,1:T(1,128)S(1)}, u32[]{:S(2)}) copy-start(s32[4096,1]{0,1:T(1,128)S(1)} %compare_select_fusion.2) | copy-start | bytes 49156
  62.6 101.1 %all-to-all-start = ((f32[1,64,128]{2,0,1:T(1,128)}), f32[1,64,128]{2,0,1:T(1,128)}, u32[]{:S(2)}, u32[]{:S(2)}) async-start(f32[1,64,128]{2,0,1:T(1,128)} %bitcast.7), calls=%async_computation | async-start | bytes 65536 | tf_op jit(solution)/shard_map/all_to_all | solution.py:75
  68.2 75.1 %all-gather.2.cloned.1.call-start = ((), (), s32[]{:S(2)}) async-start(), calls=%async_computation.2 | async-start | bytes 1310720 | tf_op jit(solution)/shard_map/all_gather | solution.py:48
  69.0 2.0 copy-start.16
  69.0 2.8 copy-start.7
  71.8 0.9 copy-start.22
  71.8 0.9 copy-start.24
  141.5 1.8 copy-start.26
  143.2 1.7 copy-start.23
  143.2 1.7 copy-start.25
  163.7 22.2 %all-to-all-start.1 = ((f32[8,64,128]{2,0,1:T(8,128)}), f32[8,64,128]{2,0,1:T(8,128)S(1)}, u32[]{:S(2)}, u32[]{:S(2)}) async-start(f32[8,64,128]{2,0,1:T(8,128)} %copy.94), calls=%async_computation.1 | async-start | bytes 524288 | tf_op jit(solution)/shard_map/all_to_all | solution.py:68
  235.0 1.7 copy-start.4
  235.0 3.7 %copy-start.5 = (f32[5,5,2048]{2,1,0:T(8,128)S(1)}, f32[5,5,2048]{2,1,0:T(8,128)}, u32[]{:S(2)}) copy-start(f32[5,5,2048]{2,1,0:T(8,128)} %param.24) | copy-start | bytes 614404
  236.7 2.5 copy-start.11
  239.2 2.7 copy-start.19
  249.8 11.3 %collective-permute-start.4 = (f32[20,256]{0,1:T(8,128)}, f32[20,256]{0,1:T(8,128)}, u32[]{:S(2)}, u32[]{:S(2)}) collective-permute-start(f32[20,256]{0,1:T(8,128)} %get-tuple-element.14), channel_id=1, source_target_pairs={{0,4},{4,8},{8,12},{12,16},{16,20},{20,24},{24,28},{28,32},{32,36}... | collective-permute-start | bytes 61448 | tf_op jit(solution)/shard_map/ppermute | solution.py:11
  250.8 11.3 %collective-permute-start.5 = (f32[20,256]{0,1:T(8,128)}, f32[20,256]{0,1:T(8,128)S(1)}, u32[]{:S(2)}, u32[]{:S(2)}) collective-permute-start(f32[20,256]{0,1:T(8,128)} %get-tuple-element.13), channel_id=1, source_target_pairs={{0,252},{4,0},{8,4},{12,8},{16,12},{20,16},{24,20},{28,24},{32,28}... | collective-permute-start | bytes 61448 | tf_op jit(solution)/shard_map/ppermute | solution.py:11
  255.8 8.5 %collective-permute-start.6 = (f32[20,256]{0,1:T(8,128)}, f32[20,256]{0,1:T(8,128)S(1)}, u32[]{:S(2)}, u32[]{:S(2)}) collective-permute-start(f32[20,256]{0,1:T(8,128)} %get-tuple-element.12), channel_id=1, source_target_pairs={{0,8},{4,12},{8,16},{12,20},{16,24},{20,28},{24,32},{28,36},{32,40... | collective-permute-start | bytes 61448 | tf_op jit(solution)/shard_map/ppermute | solution.py:11
  255.8 8.5 %collective-permute-start.7 = (f32[20,256]{0,1:T(8,128)}, f32[20,256]{0,1:T(8,128)S(1)}, u32[]{:S(2)}, u32[]{:S(2)}) collective-permute-start(f32[20,256]{0,1:T(8,128)} %get-tuple-element.11), channel_id=1, source_target_pairs={{0,248},{4,252},{8,0},{12,4},{16,8},{20,12},{24,16},{28,20},{32,24... | collective-permute-start | bytes 61448 | tf_op jit(solution)/shard_map/ppermute | solution.py:11
  327.6 1.1 copy-start.8
  327.6 1.1 copy-start.9
  327.7 1.1 copy-start.10
  327.7 1.1 copy-start.12
  327.7 1.1 copy-start.13
  327.7 1.3 copy-start.6
  327.7 2.2 copy-start.1
Sparse Core Ops, SparseCore 0:
  70.8 26.6 all-gather.1
where the time goes:
time: 340 us; the launch traced here: 337 us
  local copies, waits for them, and re-layouts  172 us (51%)
  other arithmetic  96.2 us (28%)
  starting transfers between devices  39.3 us (12%)
  between operations  14.2 us (4%)
  waiting for transfers between devices  13.9 us (4%)
    gather x2, local copies, waits for them, and re-layouts, shards(): jnp.take(extended, neighbor_flat, axis=1)  90.1 us
    scatter-add x1, other arithmetic, shards(): wall_sum = jnp.zeros((4 * pair_dev, cell_count), jnp.float32).at[:, cell_...  44.8 us
    ppermute x8, starting transfers between devices, from_behind(): lax.ppermute(value, axis, [(i, (i + by) % length) for i in range(length)])  23.3 us
    unnamed x68, local copies, waits for them, and re-layouts  22 us
    select_n x2, other arithmetic, shards(): jnp.take(extended, neighbor_flat, axis=1)  20.7 us
    another operation x3, other arithmetic  19 us
    scatter x1, local copies, waits for them, and re-layouts, shards(): jnp.zeros((4 * pair_dev, dom_size * capacity), jnp.float32).at[:, slot_flat]  13.1 us
    all_to_all x1, waiting for transfers between devices, shards(): lax.all_to_all(send_values.reshape(4 * pair_dev, dom_size, capacity), 'do...  11.2 us
  transfers between devices with their start and end apart: 11, of which 2 were waited for; matrix products, arithmetic and copies ran while one was open for 40% of the time, Pallas kernels for 0%

commit v1 on v0

v1 whole, which is shorter than its diff:
```python
import jax
import jax.numpy as jnp
from jax import lax
from jax.experimental import pallas as pl
from jax.experimental.pallas import tpu as pltpu
from jax.sharding import PartitionSpec as P

SWEEPS = 2
F32 = jnp.float32
BF16 = jnp.bfloat16
LANES = 128
NT = (((1,), (1,)), ((), ()))


def from_behind(value, axis, by):
    length = lax.axis_size(axis)
    return lax.ppermute(value, axis, [(i, (i + by) % length) for i in range(length)])


def kernel_call(body, outs, scratch=()):
    return pl.pallas_call(
        body,
        out_shape=[jax.ShapeDtypeStruct(shape, dtype) for shape, dtype in outs],
        scratch_shapes=list(scratch),
        compiler_params=pltpu.CompilerParams(vmem_limit_bytes=56 << 20),
    )


def bcast(ref, row, rows=8):
    return ref[pl.ds(row, rows, stride=0), :]


def face_kernel(coef_ref, spline_ref, out_ref):
    coef = coef_ref[...]
    blocks = spline_ref.shape[0]
    for k in range(blocks):
        for q in range(2):
            v = jnp.dot(coef, spline_ref[k, q], preferred_element_type=F32)
            for y in range(4):
                out_ref[y, q * 4 : q * 4 + 4, k * LANES : (k + 1) * LANES] = v[y * 4 : y * 4 + 4]


def dispatch_kernel(vals_ref, dest_ref, cell_ref, out_ref, o_ref, a_ref, b_ref):
    doms = out_ref.shape[0] // 9
    tiles = dest_ref.shape[0]
    iota_d = lax.broadcasted_iota(jnp.int32, (doms, LANES), 0)
    iota_p = lax.broadcasted_iota(jnp.int32, (LANES, LANES), 0)
    iota_l = lax.broadcasted_iota(jnp.int32, (LANES, LANES), 1)
    upper = jnp.concatenate(
        [jnp.where(iota_p <= iota_l, 1.0, 0.0), jnp.ones((LANES, LANES), F32)], axis=1
    ).astype(BF16)
    for t in range(tiles):
        o_ref[t * doms : (t + 1) * doms, :] = jnp.where(
            iota_d == bcast(dest_ref, t, doms), 1.0, 0.0
        ).astype(BF16)
    carry = jnp.zeros((doms, LANES), F32)
    per_rep = tiles // 4
    for t in range(tiles):
        one = o_ref[t * doms : (t + 1) * doms, :]
        counts = jnp.dot(one, upper, preferred_element_type=F32)
        place = counts[:, :LANES] + carry
        carry = carry + counts[:, LANES:]
        pos = jnp.sum(one.astype(F32) * place, axis=0, keepdims=True).astype(jnp.int32) - 1
        lanes = slice(t * LANES, (t + 1) * LANES)
        b_ref[:, lanes] = jnp.where(iota_p == pos, 1.0, 0.0).astype(BF16)
        part = slice((t % per_rep) * LANES, (t % per_rep + 1) * LANES)
        v8 = vals_ref[t // per_rep, :, part]
        hi8 = v8.astype(BF16).astype(F32)
        lo8 = v8 - hi8
        for v in range(8):
            hi = jnp.broadcast_to(hi8[v : v + 1], (doms, LANES)).astype(BF16)
            lo = jnp.broadcast_to(lo8[v : v + 1], (doms, LANES)).astype(BF16)
            a_ref[v * doms : (v + 1) * doms, lanes] = hi * one
            a_ref[(9 + v) * doms : (10 + v) * doms, lanes] = lo * one
        cell = bcast(cell_ref, t, doms)
        a_ref[8 * doms : 9 * doms, lanes] = ((cell >> 7) << 7).astype(F32).astype(BF16) * one
        a_ref[17 * doms : 18 * doms, lanes] = (cell & 127).astype(F32).astype(BF16) * one
    acc = lax.dot_general(a_ref[...], b_ref[...], NT, preferred_element_type=F32)
    for v in range(9):
        out_ref[pl.ds(v, doms, stride=9), :] = (
            acc[v * doms : (v + 1) * doms] + acc[(9 + v) * doms : (10 + v) * doms]
        )


def field_row(f, t):
    return (f // 2) * 32 + t * 2 + f % 2


def load_half(ref, f, h):
    return ref[pl.ds(field_row(f, 8 * h), 8, stride=2), :]


def store_half(ref, f, h, value):
    ref[pl.ds(field_row(f, 8 * h), 8, stride=2), :] = value


def lane_take(row, lanes):
    return jnp.take_along_axis(row, lanes, axis=1, mode="promise_in_bounds")


def pick_rows(src_ref, send_ref, out_refs):
    idx = send_ref[...]
    hi, lo = idx >> 7, idx & 127
    masks = [hi == t for t in range(16)]
    for f in range(20):
        acc = lane_take(bcast(src_ref, field_row(f, 0)), lo)
        for t in range(1, 16):
            acc = jnp.where(masks[t], lane_take(bcast(src_ref, field_row(f, t)), lo), acc)
        for k in range(4):
            out_refs[k][f * 2 : f * 2 + 2, :] = acc[2 * k : 2 * k + 2]


def pick_kernel(src_ref, send_ref, *out_refs):
    pick_rows(src_ref, send_ref, out_refs)


def couple(h, src_ref, ghost_refs, near_ref, jac_ref):
    coupling = [None] * 20
    for j in range(6):
        idx = near_ref[j * 16 + h * 8 : j * 16 + h * 8 + 8, :]
        hi, lo = idx >> 7, idx & 127
        masks = [hi == t for t in range(24)]
        for g in range(5):
            beside = []
            for rp in range(4):
                f = g * 4 + rp
                acc = lane_take(bcast(src_ref, field_row(f, 0)), lo)
                for t in range(1, 16):
                    acc = jnp.where(masks[t], lane_take(bcast(src_ref, field_row(f, t)), lo), acc)
                for t in range(8):
                    row = bcast(ghost_refs[t // 2], f * 2 + t % 2)
                    acc = jnp.where(masks[16 + t], lane_take(row, lo), acc)
                beside.append(acc)
            for e in range(5):
                row = ((j * 5 + e) * 5 + g) * 16 + h * 8
                jac = jac_ref[row : row + 8, :]
                for rp in range(4):
                    term = jac * beside[rp]
                    at = e * 4 + rp
                    coupling[at] = term if coupling[at] is None else coupling[at] + term
    return coupling


def add_spin(h, coupling, src_ref, freq):
    for g in range(5):
        for p in range(2):
            re, im = g * 4 + p, g * 4 + 2 + p
            coupling[re] = coupling[re] - freq[p] * load_half(src_ref, im, h)
            coupling[im] = coupling[im] + freq[p] * load_half(src_ref, re, h)


def own_freq(freq_ref):
    first = lax.axis_index("rep") * 2
    return [freq_ref[first], freq_ref[first + 1]]


def solve(h, diag_ref, e, rp, parts):
    total = None
    for g in range(5):
        row = (e * 5 + g) * 16 + h * 8
        term = diag_ref[row : row + 8, :] * parts[g * 4 + rp]
        total = term if total is None else total + term
    return total


def first_kernel(freq_ref, src_ref, g0, g1, g2, g3, near_ref, jac_ref, diag_ref, flow_ref, weight_ref, pre_ref, base_ref, map_ref):
    freq = own_freq(freq_ref)
    for h in range(2):
        flow = [load_half(flow_ref, f, h) for f in range(20)]
        for e in range(5):
            for rp in range(4):
                store_half(base_ref, e * 4 + rp, h, solve(h, diag_ref, e, rp, flow))
        for q in range(2):
            weight = [None] * 20
            for g in range(5):
                weight[g * 4] = weight_ref[pl.ds(g * 32 + h * 16 + q, 8, stride=2), :]
            for e in range(5):
                row = (e * 2 + q) * 16 + h * 8
                map_ref[row : row + 8, :] = solve(h, diag_ref, e, 0, weight)
        coupling = couple(h, src_ref, (g0, g1, g2, g3), near_ref, jac_ref)
        add_spin(h, coupling, src_ref, freq)
        for e in range(5):
            for rp in range(4):
                f = e * 4 + rp
                store_half(pre_ref, f, h, load_half(base_ref, f, h) - solve(h, diag_ref, e, rp, coupling))


def wall_kernel(freq_ref, recv_ref, send_ref, pre_ref, base_ref, map_ref, it_ref, rhs_ref, h0, h1, h2, h3, a_ref, b_ref):
    freq = own_freq(freq_ref)
    sources = recv_ref.shape[0] // 9
    iota16 = lax.broadcasted_iota(jnp.int32, (16, LANES), 0)
    iota_l = lax.broadcasted_iota(jnp.int32, (LANES, LANES), 0)
    for s in range(sources):
        lanes = slice(s * LANES, (s + 1) * LANES)
        cell = bcast(recv_ref, s * 9 + 8).astype(jnp.int32)
        tile, lane = cell >> 7, cell & 127
        mask = jnp.where(iota16 == jnp.concatenate([tile] * 2, 0), 1.0, 0.0).astype(BF16)
        b_ref[:, lanes] = jnp.where(iota_l == jnp.concatenate([lane] * 16, 0), 1.0, 0.0).astype(BF16)
        for v in range(8):
            x = bcast(recv_ref, s * 9 + v)
            hi = x.astype(BF16)
            lo = (x - hi.astype(F32)).astype(BF16)
            a_ref[v * 16 : v * 16 + 16, lanes] = jnp.concatenate([hi, hi], 0) * mask
            a_ref[LANES + v * 16 : LANES + v * 16 + 16, lanes] = jnp.concatenate([lo, lo], 0) * mask
    both = lax.dot_general(a_ref[...], b_ref[...], NT, preferred_element_type=F32)
    wall = both[:LANES] + both[LANES:]
    for h in range(2):
        w = [wall[v * 16 + h * 8 : v * 16 + h * 8 + 8] for v in range(8)]
        velocity = [-freq[0] * w[2], -freq[1] * w[3], freq[0] * w[0], freq[1] * w[1]]
        for e in range(5):
            m0 = map_ref[e * 32 + h * 8 : e * 32 + h * 8 + 8, :]
            m1 = map_ref[e * 32 + 16 + h * 8 : e * 32 + 24 + h * 8, :]
            for rp in range(4):
                f = e * 4 + rp
                term = m0 * velocity[rp] + m1 * w[4 + rp]
                store_half(it_ref, f, h, load_half(pre_ref, f, h) + term)
                store_half(rhs_ref, f, h, load_half(base_ref, f, h) + term)
    pick_rows(it_ref, send_ref, (h0, h1, h2, h3))


def last_kernel(freq_ref, src_ref, g0, g1, g2, g3, near_ref, jac_ref, diag_ref, rhs_ref, out_ref):
    freq = own_freq(freq_ref)
    for h in range(2):
        coupling = couple(h, src_ref, (g0, g1, g2, g3), near_ref, jac_ref)
        add_spin(h, coupling, src_ref, freq)
        for e in range(5):
            for rp in range(4):
                f = e * 4 + rp
                store_half(out_ref, f, h, load_half(rhs_ref, f, h) - solve(h, diag_ref, e, rp, coupling))


def smem_call(body, operands, outs, scratch=()):
    specs = [pl.BlockSpec(memory_space=pltpu.SMEM)] + [pl.BlockSpec(memory_space=pltpu.VMEM)] * (
        len(operands) - 1
    )
    return pl.pallas_call(
        body,
        out_shape=[jax.ShapeDtypeStruct(shape, dtype) for shape, dtype in outs],
        in_specs=specs,
        scratch_shapes=list(scratch),
        compiler_params=pltpu.CompilerParams(vmem_limit_bytes=56 << 20),
    )(*operands)


def to_rows(field):
    lead = field.shape[:-2]
    inner = field.reshape(*lead, 2, field.shape[-1] // LANES, LANES)
    return jnp.swapaxes(inner, -3, -2).reshape(-1, LANES)


def from_rows(rows, shape):
    inner = rows.reshape(*shape[:-2], shape[-1] // LANES, 2, LANES)
    return jnp.swapaxes(inner, -3, -2).reshape(shape)


def exchange(blocks):
    return [
        from_behind(block, "dom", by) for block, by in zip(blocks, (1, -1, 2, -2), strict=True)
    ]


def shards(
    spline_blocks,
    modal_coeff,
    frequency,
    face_dest,
    face_cell,
    wall_weight,
    flow_rhs,
    previous,
    diag_inverse,
    off_jacobian,
    neighbor,
    send_list,
):
    dom = lax.axis_size("dom")
    halo = [((40, LANES), F32)] * 4
    coef = modal_coeff.reshape(64, 2, 4, 2).transpose(2, 1, 3, 0).reshape(16, 64)
    faces = kernel_call(face_kernel, [((4, 8, 1024), F32)])(coef, spline_blocks)[0]
    faces = lax.all_to_all(faces, "rep", split_axis=0, concat_axis=0, tiled=True)
    send = kernel_call(
        dispatch_kernel,
        [((dom * 9, LANES), F32)],
        [
            pltpu.VMEM((32 * dom, LANES), BF16),
            pltpu.VMEM((18 * dom, 4096), BF16),
            pltpu.VMEM((LANES, 4096), BF16),
        ],
    )(faces, face_dest.reshape(32, LANES), face_cell.reshape(32, LANES))[0]
    recv = lax.all_to_all(send, "dom", split_axis=0, concat_axis=0, tiled=True)

    prev = to_rows(previous)
    rows_out = send_list.reshape(8, LANES)
    picked = kernel_call(pick_kernel, halo)(prev, rows_out)
    ghosts = exchange(picked)
    near = neighbor.reshape(96, LANES)
    jac = off_jacobian.astype(F32).reshape(2400, LANES)
    diag = diag_inverse.reshape(400, LANES)
    field = ((320, LANES), F32)
    pre, base, wall_map = smem_call(
        first_kernel,
        (frequency, prev, *ghosts, near, jac, diag, to_rows(flow_rhs), to_rows(wall_weight)),
        [field, field, ((160, LANES), F32)],
    )
    it, rhs, *picked = smem_call(
        wall_kernel,
        (frequency, recv, rows_out, pre, base, wall_map),
        [field, field, *halo],
        [pltpu.VMEM((2 * LANES, dom * LANES), BF16), pltpu.VMEM((LANES, dom * LANES), BF16)],
    )
    ghosts = exchange(picked)
    out = smem_call(last_kernel, (frequency, it, *ghosts, near, jac, diag, rhs), [field])[0]
    return from_rows(out, flow_rhs.shape)


def solution(mesh):
    return jax.shard_map(
        shards,
        mesh=mesh,
        in_specs=(
            P(("dom", "rep"), None, None, None),
            P(),
            P(),
            P("dom", None),
            P("dom"),
            P(None, None, "dom"),
            P(None, None, "rep", "dom"),
            P(None, None, "rep", "dom"),
            P(None, None, "dom"),
            P(None, None, None, "dom"),
            P(None, "dom"),
            P(None, "dom"),
        ),
        out_specs=P(None, None, "rep", "dom"),
        check_vma=False,
    )
```

time: 340 us -> 86.1 us (0.25)
  local copies, waits for them, and re-layouts: 172 us -> 9.02 us
  other arithmetic: 96.2 us -> 0 us
  Pallas kernels: 0 us -> 31.2 us
  between operations: 14.2 us -> 0.11 us
  waiting for transfers between devices: 13.9 us -> 2.98 us
  blocking collectives: 0 us -> 10.7 us
  starting transfers between devices: 39.3 us -> 31.6 us
    gather x4 -> x0, local copies, waits for them, and re-layouts: 98.1 us -> none  [the longest x2 90.1 us: shards(): jnp.take(extended, neighbor_flat, axis=1)]
    scatter-add x1 -> x0, other arithmetic: 44.8 us -> none  [shards(): wall_sum = jnp.zeros((4 * pair_dev, cell_count), jnp.float32).at[:, cell_...]
    pallas_call x0 -> x6, Pallas kernels: none -> 31.2 us  [the longest x3 22.4 us: smem_call(): pl.pallas_call(body, out_shape=[jax.ShapeDtypeStruct(shape, dtype) for sh...]
    select_n x6 -> x0, other arithmetic: 23 us -> none  [the longest x2 20.7 us: shards(): jnp.take(extended, neighbor_flat, axis=1)]
    unnamed x68 -> x24, local copies, waits for them, and re-layouts: 22 us -> 1.22 us
    another operation x7 -> x0, other arithmetic: 19.2 us -> none
    scatter x1 -> x0, local copies, waits for them, and re-layouts: 13.1 us -> none  [shards(): jnp.zeros((4 * pair_dev, dom_size * capacity), jnp.float32).at[:, slot_flat]]
    all_to_all x2 -> x1, waiting for transfers between devices: 11.2 us -> 0.01 us  [shards(): recv = lax.all_to_all(send, 'dom', split_axis=0, concat_axis=0, tiled=True)]
  transfers between devices with their start and end apart: 11 -> 9, of which waited for: 2 -> 2; matrix products, arithmetic and copies ran while one was open for 40% -> 5% of each run, Pallas kernels for 0% -> 13%
where the time goes in v1:
time: 86.1 us; the launch traced here: 85.6 us
  starting transfers between devices  31.6 us (37%)
  Pallas kernels  31.2 us (36%)
  blocking collectives  10.7 us (12%)
  local copies, waits for them, and re-layouts  9.02 us (10%)
  waiting for transfers between devices  2.98 us (3%)
    pallas_call x3, Pallas kernels, smem_call(): pl.pallas_call(body, out_shape=[jax.ShapeDtypeStruct(shape, dtype) for sh...  22.4 us
    ppermute x8, starting transfers between devices, from_behind(): lax.ppermute(value, axis, [(i, (i + by) % length) for i in range(length)])  20.8 us
    all_to_all x1, starting transfers between devices, shards(): recv = lax.all_to_all(send, 'dom', split_axis=0, concat_axis=0, tiled=True)  10.8 us
    all_to_all x1, blocking collectives, shards(): lax.all_to_all(faces, 'rep', split_axis=0, concat_axis=0, tiled=True)  10.7 us
    pallas_call x1, Pallas kernels, shards(): kernel_call(dispatch_kernel, [((dom * 9, LANES), F32)], [pltpu.VMEM((32 *...  5.05 us
    ppermute x8, waiting for transfers between devices, from_behind(): lax.ppermute(value, axis, [(i, (i + by) % length) for i in range(length)])  2.98 us
    all_to_all x2, local copies, waits for them, and re-layouts, shards(): recv = lax.all_to_all(send, 'dom', split_axis=0, concat_axis=0, tiled=True)  2.52 us
    pallas_call x1, Pallas kernels, shards(): picked = kernel_call(pick_kernel, halo)(prev, rows_out)  1.95 us
  transfers between devices with their start and end apart: 9, of which 2 were waited for; matrix products, arithmetic and copies ran while one was open for 5% of the time, Pallas kernels for 13%

profile of v1, /device:TPU:8, one launch (start us, length us, event | category | flops | bytes accessed | tf_op | source)
XLA Modules:
  0.0 85.6 jit_solution(12035744216190182151)
XLA Ops:
  0.0 0.0 copy-start.11
  0.0 0.0 copy-start
  0.0 1.4 %copy.19 = bf16[64,2,4,2]{0,3,1,2:T(2,128)(2,1)} copy(bf16[64,2,4,2]{0,3,2,1:T(2,128)(2,1)} %bitcast.33) | data formatting | bytes 4096 | tf_op jit(solution)/shard_map/reshape | solution.py:278
  1.4 1.8 %shard_map.118 = f32[4,8,1024]{2,1,0:T(8,128)} custom-call(bf16[16,64]{1,0:T(8,128)(2,1)} %bitcast.30, bf16[8,2,64,128]{3,2,1,0:T(8,128)(2,1)} %spline_ref.1), custom_call_target="tpu_custom_call" | custom-call | tf_op jit(solution)/shard_map/pallas_call | solution.py:279
  3.2 10.7 %all_to_all.16.vals_ref = f32[4,8,1024]{2,1,0:T(8,128)} all-to-all(f32[4,8,1024]{2,1,0:T(8,128)} %shard_map.118), channel_id=1, replica_groups=mesh['dom'=64,'rep'=4] {'rep'}, dimensions={0} | all-to-all | bytes 262144 | tf_op jit(solution)/shard_map/all_to_all | solution.py:280
  13.8 5.1 %shard_map.119 = f32[576,128]{1,0:T(8,128)} custom-call(f32[4,8,1024]{2,1,0:T(8,128)} %all_to_all.16.vals_ref, s32[32,128]{1,0:T(8,128)} %bitcast.31, s32[32,128]{1,0:T(8,128)} %bitcast.32), custom_call_target="tpu_custom_call" | custom-call | tf_op jit(solution)/shard_map/pallas_call | solution.py:281
  18.9 1.8 %all_to_all.11 = f32[64,9,128]{2,1,0:T(8,128)} reshape(f32[576,128]{1,0:T(8,128)} %shard_map.119) | data formatting | bytes 589824 | tf_op jit(solution)/shard_map/all_to_all | solution.py:290
  20.7 10.8 %all-to-all-start.1 = ((f32[64,9,128]{2,1,0:T(8,128)}), f32[64,9,128]{2,1,0:T(8,128)S(1)}, u32[]{:S(2)}, u32[]{:S(2)}) async-start(f32[64,9,128]{2,1,0:T(8,128)} %all_to_all.11), calls=%async_computation.1 | async-start | bytes 1048576 | tf_op jit(solution)/shard_map/all_to_all | solution.py:290
  31.5 0.0 copy-done.11
  31.5 0.6 reshape.56.send_ref
  32.1 1.9 %shard_map.120 = (f32[40,128]{1,0:T(8,128)}, f32[40,128]{1,0:T(8,128)}, f32[40,128]{1,0:T(8,128)}, f32[40,128]{1,0:T(8,128)}) custom-call(f32[320,128]{1,0:T(8,128)} %bitcast.26, s32[8,128]{1,0:T(8,128)} %reshape.56.send_ref), custom_call_target="tpu_custom_call" | custom-call | tf_op jit(solution)/shard_map/pallas_call | solution.py:294
  34.0 0.1 collective-permute-start
  34.1 5.0 %collective-permute-start.1 = (f32[40,128]{1,0:T(8,128)}, f32[40,128]{1,0:T(8,128)S(1)}, u32[]{:S(2)}, u32[]{:S(2)}) collective-permute-start(f32[40,128]{1,0:T(8,128)} %get-tuple-element.19), channel_id=1, source_target_pairs={{0,252},{4,0},{8,4},{12,8},{16,12},{20,16},{24,20},{28,24},{32,28}... | collective-permute-start | bytes 61448 | tf_op jit(solution)/shard_map/ppermute | solution.py:17
  39.1 0.0 collective-permute-start.2
  39.1 5.3 %collective-permute-start.3 = (f32[40,128]{1,0:T(8,128)}, f32[40,128]{1,0:T(8,128)S(1)}, u32[]{:S(2)}, u32[]{:S(2)}) collective-permute-start(f32[40,128]{1,0:T(8,128)} %get-tuple-element.21), channel_id=1, source_target_pairs={{0,248},{4,252},{8,0},{12,4},{16,8},{20,12},{24,16},{28,20},{32,24... | collective-permute-start | bytes 61448 | tf_op jit(solution)/shard_map/ppermute | solution.py:17
  44.4 0.0 copy-done
  44.4 0.4 copy.21
  44.8 0.0 copy-start.1
  44.8 0.0 copy-start.2
  44.9 1.5 %reshape.70.jac_ref = f32[2400,128]{1,0:T(8,128)} reshape(f32[6,5,5,2048]{3,2,1,0:T(8,128)S(1)} %copy.21) | data formatting | bytes 2457600 | tf_op jit(solution)/shard_map/reshape | solution.py:297
  46.4 0.0 copy-done.1
  46.4 0.8 reshape.62.diag_ref
  47.2 0.0 copy-done.2
  47.2 0.6 reshape.59.near_ref
  47.8 0.0 collective-permute-done.g0
  47.8 0.0 copy-start.3
  47.8 0.0 collective-permute-done.1.g1
  47.8 0.0 copy-start.4
  47.8 1.0 %collective-permute-done.2.g2 = f32[40,128]{1,0:T(8,128)S(1)} collective-permute-done((f32[40,128]{1,0:T(8,128)}, f32[40,128]{1,0:T(8,128)S(1)}, u32[]{:S(2)}, u32[]{:S(2)}) %collective-permute-start.2) | collective-permute-done | bytes 20512 | tf_op jit(solution)/shard_map/ppermute | solution.py:17
  48.8 0.0 copy-start.6
  48.8 0.0 collective-permute-done.3.g3
  48.8 0.0 copy-start.9
  48.8 0.0 copy-done.3
  48.9 0.0 copy-done.4
  48.9 0.6 copy-done.6
  49.4 0.0 copy-done.9
  49.5 8.8 %shard_map.121 = (f32[320,128]{1,0:T(8,128)}, f32[320,128]{1,0:T(8,128)}, f32[160,128]{1,0:T(8,128)}) custom-call(f32[8]{0:T(128)} %freq_ref.5, f32[320,128]{1,0:T(8,128)} %bitcast.27, f32[40,128]{1,0:T(8,128)} %copy-done.3, f32[40,128]{1,0:T(8,128)} %copy-done.4, f32[40,128]{1,0:T(8,128)} %copy-done.6, f32[40,128]{1,0:T(8,128)} %copy-done.9, ...), custom_call_target="tpu_custom_call" | custom-call | tf_op jit(solution)/shard_map/pallas_call | solution.py:236
  58.2 0.0 all-to-all-done.1
  58.2 0.7 all_to_all.13.recv_ref
  59.0 4.9 %shard_map.122 = (f32[320,128]{1,0:T(8,128)}, f32[320,128]{1,0:T(8,128)}, f32[40,128]{1,0:T(8,128)}, f32[40,128]{1,0:T(8,128)}, f32[40,128]{1,0:T(8,128)}, /*index=5*/f32[40,128]{1,0:T(8,128)}) custom-call(f32[8]{0:T(128)} %freq_ref.5, f32[576,128]{1,0:T(8,128)} %all_to_all.13.recv_ref, s32[8,128]{1,0:T(8,128)} %reshape.56.send_ref, ...), custom_call_target="tpu_custom_call" | custom-call | tf_op jit(solution)/shard_map/pallas_call | solution.py:236
  63.9 0.0 collective-permute-start.4
  63.9 5.1 %collective-permute-start.5 = (f32[40,128]{1,0:T(8,128)}, f32[40,128]{1,0:T(8,128)S(1)}, u32[]{:S(2)}, u32[]{:S(2)}) collective-permute-start(f32[40,128]{1,0:T(8,128)} %get-tuple-element.27), channel_id=1, source_target_pairs={{0,252},{4,0},{8,4},{12,8},{16,12},{20,16},{24,20},{28,24},{32,28}... | collective-permute-start | bytes 61448 | tf_op jit(solution)/shard_map/ppermute | solution.py:17
  68.9 0.0 collective-permute-start.6
  68.9 5.3 %collective-permute-start.7 = (f32[40,128]{1,0:T(8,128)}, f32[40,128]{1,0:T(8,128)S(1)}, u32[]{:S(2)}, u32[]{:S(2)}) collective-permute-start(f32[40,128]{1,0:T(8,128)} %get-tuple-element.29), channel_id=1, source_target_pairs={{0,248},{4,252},{8,0},{12,4},{16,8},{20,12},{24,16},{28,20},{32,24... | collective-permute-start | bytes 61448 | tf_op jit(solution)/shard_map/ppermute | solution.py:17
  74.3 0.0 collective-permute-done.4.g0
  74.3 0.0 copy-start.5
  74.3 0.0 collective-permute-done.5.g1
  74.3 0.0 copy-start.7
  74.3 1.9 %collective-permute-done.6.g2 = f32[40,128]{1,0:T(8,128)S(1)} collective-permute-done((f32[40,128]{1,0:T(8,128)}, f32[40,128]{1,0:T(8,128)S(1)}, u32[]{:S(2)}, u32[]{:S(2)}) %collective-permute-start.6) | collective-permute-done | bytes 20512 | tf_op jit(solution)/shard_map/ppermute | solution.py:17
  76.2 0.0 copy-start.8
  76.2 0.0 collective-permute-done.7.g3
  76.2 0.0 copy-start.10
  76.2 0.0 copy-done.5
  76.3 0.0 copy-done.7
  76.3 0.6 copy-done.8
  76.8 0.0 copy-done.10
  76.9 8.8 %shard_map.123 = f32[320,128]{1,0:T(8,128)} custom-call(f32[8]{0:T(128)} %freq_ref.5, f32[320,128]{1,0:T(8,128)} %get-tuple-element.25.src_ref, f32[40,128]{1,0:T(8,128)} %copy-done.5, f32[40,128]{1,0:T(8,128)} %copy-done.7, f32[40,128]{1,0:T(8,128)} %copy-done.8, f32[40,128]{1,0:T(8,128)} %copy-done.10, s32[96,128]{1,0:T(8,128)} %reshape.59.near_ref, ...), custom_call_target="tpu_custom_call" | custom-call | tf_op jit(solution)/shard_map/pallas_call | solution.py:236
Async XLA Ops:
  0.0 31.5 %copy-start.11 = (s32[4,256]{1,0:T(4,128)S(1)}, s32[4,256]{1,0:T(4,128)}, u32[]{:S(2)}) copy-start(s32[4,256]{1,0:T(4,128)} %param.23) | copy-start | bytes 12292
  0.0 44.4 %copy-start = (bf16[6,5,5,2048]{3,0,2,1:T(8,128)(2,1)S(1)}, bf16[6,5,5,2048]{3,0,2,1:T(8,128)(2,1)}, u32[]{:S(2)}) copy-start(bf16[6,5,5,2048]{3,0,2,1:T(8,128)(2,1)} %param.21) | copy-start | bytes 1843204
  20.7 37.6 %all-to-all-start.1 = ((f32[64,9,128]{2,1,0:T(8,128)}), f32[64,9,128]{2,1,0:T(8,128)S(1)}, u32[]{:S(2)}, u32[]{:S(2)}) async-start(f32[64,9,128]{2,1,0:T(8,128)} %all_to_all.11), calls=%async_computation.1 | async-start | bytes 1048576 | tf_op jit(solution)/shard_map/all_to_all | solution.py:290
  34.0 13.8 %collective-permute-start = (f32[40,128]{1,0:T(8,128)}, f32[40,128]{1,0:T(8,128)S(1)}, u32[]{:S(2)}, u32[]{:S(2)}) collective-permute-start(f32[40,128]{1,0:T(8,128)} %get-tuple-element.18), channel_id=1, source_target_pairs={{0,4},{4,8},{8,12},{12,16},{16,20},{20,24},{24,28},{28,32},{32,36}... | collective-permute-start | bytes 61448 | tf_op jit(solution)/shard_map/ppermute | solution.py:17
  34.1 13.7 %collective-permute-start.1 = (f32[40,128]{1,0:T(8,128)}, f32[40,128]{1,0:T(8,128)S(1)}, u32[]{:S(2)}, u32[]{:S(2)}) collective-permute-start(f32[40,128]{1,0:T(8,128)} %get-tuple-element.19), channel_id=1, source_target_pairs={{0,252},{4,0},{8,4},{12,8},{16,12},{20,16},{24,20},{28,24},{32,28}... | collective-permute-start | bytes 61448 | tf_op jit(solution)/shard_map/ppermute | solution.py:17
  39.1 9.7 %collective-permute-start.2 = (f32[40,128]{1,0:T(8,128)}, f32[40,128]{1,0:T(8,128)S(1)}, u32[]{:S(2)}, u32[]{:S(2)}) collective-permute-start(f32[40,128]{1,0:T(8,128)} %get-tuple-element.20), channel_id=1, source_target_pairs={{0,8},{4,12},{8,16},{12,20},{16,24},{20,28},{24,32},{28,36},{32,40... | collective-permute-start | bytes 61448 | tf_op jit(solution)/shard_map/ppermute | solution.py:17
  39.1 9.7 %collective-permute-start.3 = (f32[40,128]{1,0:T(8,128)}, f32[40,128]{1,0:T(8,128)S(1)}, u32[]{:S(2)}, u32[]{:S(2)}) collective-permute-start(f32[40,128]{1,0:T(8,128)} %get-tuple-element.21), channel_id=1, source_target_pairs={{0,248},{4,252},{8,0},{12,4},{16,8},{20,12},{24,16},{28,20},{32,24... | collective-permute-start | bytes 61448 | tf_op jit(solution)/shard_map/ppermute | solution.py:17
  44.8 1.6 %copy-start.1 = (f32[5,5,2048]{2,1,0:T(8,128)S(1)}, f32[5,5,2048]{2,1,0:T(8,128)}, u32[]{:S(2)}) copy-start(f32[5,5,2048]{2,1,0:T(8,128)} %param.20) | copy-start | bytes 614404
  44.8 2.3 %copy-start.2 = (s32[6,2048]{1,0:T(8,128)S(1)}, s32[6,2048]{1,0:T(8,128)}, u32[]{:S(2)}) copy-start(s32[6,2048]{1,0:T(8,128)} %param.22) | copy-start | bytes 147460
  47.8 1.0 %copy-start.3 = (f32[40,128]{1,0:T(8,128)}, f32[40,128]{1,0:T(8,128)S(1)}, u32[]{:S(2)}) copy-start(f32[40,128]{1,0:T(8,128)S(1)} %collective-permute-done.g0) | copy-start | bytes 61444
  47.8 1.0 %copy-start.4 = (f32[40,128]{1,0:T(8,128)}, f32[40,128]{1,0:T(8,128)S(1)}, u32[]{:S(2)}) copy-start(f32[40,128]{1,0:T(8,128)S(1)} %collective-permute-done.1.g1) | copy-start | bytes 61444
  48.8 0.6 copy-start.6
  48.8 0.6 copy-start.9
  63.9 10.4 %collective-permute-start.4 = (f32[40,128]{1,0:T(8,128)}, f32[40,128]{1,0:T(8,128)S(1)}, u32[]{:S(2)}, u32[]{:S(2)}) collective-permute-start(f32[40,128]{1,0:T(8,128)} %get-tuple-element.26), channel_id=1, source_target_pairs={{0,4},{4,8},{8,12},{12,16},{16,20},{20,24},{24,28},{28,32},{32,36}... | collective-permute-start | bytes 61448 | tf_op jit(solution)/shard_map/ppermute | solution.py:17
  63.9 10.4 %collective-permute-start.5 = (f32[40,128]{1,0:T(8,128)}, f32[40,128]{1,0:T(8,128)S(1)}, u32[]{:S(2)}, u32[]{:S(2)}) collective-permute-start(f32[40,128]{1,0:T(8,128)} %get-tuple-element.27), channel_id=1, source_target_pairs={{0,252},{4,0},{8,4},{12,8},{16,12},{20,16},{24,20},{28,24},{32,28}... | collective-permute-start | bytes 61448 | tf_op jit(solution)/shard_map/ppermute | solution.py:17
  68.9 7.3 %collective-permute-start.6 = (f32[40,128]{1,0:T(8,128)}, f32[40,128]{1,0:T(8,128)S(1)}, u32[]{:S(2)}, u32[]{:S(2)}) collective-permute-start(f32[40,128]{1,0:T(8,128)} %get-tuple-element.28), channel_id=1, source_target_pairs={{0,8},{4,12},{8,16},{12,20},{16,24},{20,28},{24,32},{28,36},{32,40... | collective-permute-start | bytes 61448 | tf_op jit(solution)/shard_map/ppermute | solution.py:17
  68.9 7.3 %collective-permute-start.7 = (f32[40,128]{1,0:T(8,128)}, f32[40,128]{1,0:T(8,128)S(1)}, u32[]{:S(2)}, u32[]{:S(2)}) collective-permute-start(f32[40,128]{1,0:T(8,128)} %get-tuple-element.29), channel_id=1, source_target_pairs={{0,248},{4,252},{8,0},{12,4},{16,8},{20,12},{24,16},{28,20},{32,24... | collective-permute-start | bytes 61448 | tf_op jit(solution)/shard_map/ppermute | solution.py:17
  74.3 2.0 %copy-start.5 = (f32[40,128]{1,0:T(8,128)}, f32[40,128]{1,0:T(8,128)S(1)}, u32[]{:S(2)}) copy-start(f32[40,128]{1,0:T(8,128)S(1)} %collective-permute-done.4.g0) | copy-start | bytes 61444
  74.3 2.0 %copy-start.7 = (f32[40,128]{1,0:T(8,128)}, f32[40,128]{1,0:T(8,128)S(1)}, u32[]{:S(2)}) copy-start(f32[40,128]{1,0:T(8,128)S(1)} %collective-permute-done.5.g1) | copy-start | bytes 61444
  76.2 0.6 copy-start.8
  76.2 0.6 copy-start.10

commit v2 on v1

v2 whole, which is shorter than its diff:
```python
import jax
import jax.numpy as jnp
from jax import lax
from jax.experimental import pallas as pl
from jax.experimental.pallas import tpu as pltpu
from jax.sharding import PartitionSpec as P

F32 = jnp.float32
BF16 = jnp.bfloat16
LANES = 128
NT = (((1,), (1,)), ((), ()))


def from_behind(value, axis, by):
    length = lax.axis_size(axis)
    return lax.ppermute(value, axis, [(i, (i + by) % length) for i in range(length)])


def kernel_call(body, outs, scratch=()):
    return pl.pallas_call(
        body,
        out_shape=[jax.ShapeDtypeStruct(shape, dtype) for shape, dtype in outs],
        scratch_shapes=list(scratch),
        compiler_params=pltpu.CompilerParams(vmem_limit_bytes=56 << 20),
    )


def bcast(ref, row, rows=8):
    return ref[pl.ds(row, rows, stride=0), :]


def face_kernel(coef_ref, spline_ref, out_ref):
    coef = coef_ref[...]
    blocks = spline_ref.shape[0]
    for k in range(blocks):
        for q in range(2):
            v = jnp.dot(coef, spline_ref[k, q], preferred_element_type=F32)
            for y in range(4):
                for r in range(2):
                    at = q * 4 + r * 2
                    out_ref[y, at : at + 2, k * LANES : (k + 1) * LANES] = v[
                        r * 8 + y * 2 : r * 8 + y * 2 + 2
                    ]


def split_rows(x):
    hi = x.astype(BF16).astype(F32)
    return hi, x - hi


def iota_rows(rows):
    return lax.broadcasted_iota(jnp.int32, (rows, LANES), 0).astype(F32).astype(BF16)


def one_hot(iota, row16):
    full = jnp.concatenate([row16] * (iota.shape[0] // 16), 0)
    return jnp.where(iota == full, jnp.ones_like(iota), jnp.zeros_like(iota))


def slot_kernel(dest_ref, slot_ref):
    doms = 64
    tiles = dest_ref.shape[0]
    iota_d = lax.broadcasted_iota(jnp.int32, (doms, LANES), 0)
    iota_p = lax.broadcasted_iota(jnp.int32, (LANES, LANES), 0)
    iota_l = lax.broadcasted_iota(jnp.int32, (LANES, LANES), 1)
    upper = jnp.concatenate(
        [jnp.where(iota_p <= iota_l, 1.0, 0.0), jnp.ones((LANES, LANES), F32)], axis=1
    ).astype(BF16)
    carry = jnp.zeros((doms, LANES), F32)
    for t in range(tiles):
        dest = bcast(dest_ref, t, 8)
        one = jnp.where(iota_d == jnp.concatenate([dest] * 8, 0), 1.0, 0.0)
        counts = jnp.dot(one.astype(BF16), upper, preferred_element_type=F32)
        place = counts[:, :LANES] + carry
        carry = carry + counts[:, LANES:]
        rank = jnp.sum(one * place, axis=0, keepdims=True).astype(jnp.int32) - 1
        slot_ref[t : t + 1, :] = (dest[:1] & 1) * LANES + rank


def store_split(hl_ref, at, x):
    hi8, lo8 = split_rows(x)
    hl_ref[at : at + 8, :] = hi8
    hl_ref[at + 8 : at + 16, :] = lo8


def narrow(x):
    return x.astype(F32).astype(BF16)


CHUNK = 8


def add_to(total, parts_a, parts_b):
    a = jnp.concatenate([jnp.concatenate(p, axis=0) for p in parts_a], axis=1)
    b = jnp.concatenate(parts_b, axis=1)
    product = lax.dot_general(a, b, NT, preferred_element_type=F32)
    return product if total is None else total + product


def dispatch_kernel(vals_ref, dest_ref, slot_ref, cell_ref, out_ref, hl_ref):
    pairs = out_ref.shape[0] // 18
    tiles = dest_ref.shape[0]
    iota_b = iota_rows(2 * LANES)
    iota_a = iota_rows(pairs)
    per_rep = tiles // 4
    for t in range(tiles):
        part = slice((t % per_rep) * LANES, (t % per_rep + 1) * LANES)
        store_split(hl_ref, t * 16, vals_ref[t // per_rep, :, part])
    total = None
    for c in range(0, tiles, CHUNK):
        parts_a, parts_b = [], []
        for t in range(c, c + CHUNK):
            parts_b.append(one_hot(iota_b, narrow(bcast(slot_ref, t, 16))))
            mask = one_hot(iota_a, narrow(bcast(dest_ref, t, 16) >> 1))
            cell = bcast(cell_ref, t, 16)
            rows = [bcast(hl_ref, t * 16 + v, 16).astype(BF16) for v in range(16)]
            rows = rows[:8] + [narrow((cell >> 7) << 7)] + rows[8:] + [narrow(cell & 127)]
            parts_a.append([jnp.concatenate([row] * (pairs // 16), 0) * mask for row in rows])
        total = add_to(total, parts_a, parts_b)
    for v in range(9):
        both = total[v * pairs : (v + 1) * pairs] + total[(9 + v) * pairs : (10 + v) * pairs]
        for d in range(2):
            out_ref[pl.ds(d * 9 + v, pairs, stride=18), :] = both[:, d * LANES : (d + 1) * LANES]


def field_row(f, t):
    return (f // 2) * 32 + t * 2 + f % 2


def load_half(ref, f, h):
    return ref[pl.ds(field_row(f, 8 * h), 8, stride=2), :]


def store_half(ref, f, h, value):
    ref[pl.ds(field_row(f, 8 * h), 8, stride=2), :] = value


def lane_take(row, lanes):
    return jnp.take_along_axis(row, lanes, axis=1, mode="promise_in_bounds")


def pick_rows(src_ref, send_ref, out_refs):
    idx = send_ref[...]
    hi, lo = idx >> 7, idx & 127
    masks = [hi == t for t in range(16)]
    for f in range(20):
        acc = lane_take(bcast(src_ref, field_row(f, 0)), lo)
        for t in range(1, 16):
            acc = jnp.where(masks[t], lane_take(bcast(src_ref, field_row(f, t)), lo), acc)
        for k in range(4):
            out_refs[k][f * 2 : f * 2 + 2, :] = acc[2 * k : 2 * k + 2]


def pick_kernel(src_ref, send_ref, *out_refs):
    pick_rows(src_ref, send_ref, out_refs)


def part_row(f):
    return (f // 2) * 16 + f % 2


def load_part(ref, f):
    return ref[pl.ds(part_row(f), 8, stride=2), :]


def store_part(ref, f, value):
    ref[pl.ds(part_row(f), 8, stride=2), :] = value


def couple(first_tile, rows_of, near_ref, jac_ref, beside_ref):
    coupling = [None] * 20
    tiles = len(rows_of(0))
    for step_at in range(7):
        if step_at < 6:
            idx = near_ref[step_at * 8 : step_at * 8 + 8, :]
            hi, lo = idx >> 7, idx & 127
            masks = [hi == first_tile + t for t in range(tiles)]
            for f in range(20):
                acc = jnp.zeros((8, LANES), F32)
                for t, (ref, row) in enumerate(rows_of(f)):
                    acc = jnp.where(masks[t], lane_take(bcast(ref, row), lo), acc)
                beside_ref[(step_at * 20 + f) * 8 : (step_at * 20 + f) * 8 + 8, :] = acc
        j = step_at - 1
        if j >= 0:
            for g in range(5):
                at = (j * 20 + g * 4) * 8
                beside = [beside_ref[at + rp * 8 : at + rp * 8 + 8, :] for rp in range(4)]
                for e in range(5):
                    row = ((j * 5 + e) * 5 + g) * 8
                    jac = jac_ref[row : row + 8, :]
                    for rp in range(4):
                        term = jac * beside[rp]
                        at_e = e * 4 + rp
                        coupling[at_e] = term if coupling[at_e] is None else coupling[at_e] + term
    return coupling


def local_coupling(h, freq, src_ref, near_ref, jac_ref, beside_ref):
    coupling = couple(0, lambda f: [(src_ref, field_row(f, t)) for t in range(16)], near_ref, jac_ref, beside_ref)
    for g in range(5):
        for p in range(2):
            re, im = g * 4 + p, g * 4 + 2 + p
            coupling[re] = coupling[re] - freq[p] * load_half(src_ref, im, h)
            coupling[im] = coupling[im] + freq[p] * load_half(src_ref, re, h)
    return coupling


def own_freq(freq_ref):
    first = lax.axis_index("rep") * 2
    return [freq_ref[first], freq_ref[first + 1]]


def solve(diag_ref, e, rp, parts):
    total = None
    for g in range(5):
        row = (e * 5 + g) * 8
        term = diag_ref[row : row + 8, :] * parts[g * 4 + rp]
        total = term if total is None else total + term
    return total


def untile(tables_ref, base, tiles_of, count, tile_count, write):
    for t in range(tile_count):
        tables_ref[base + t * 8 : base + t * 8 + count, :] = tiles_of(slice(t * LANES, (t + 1) * LANES))
    for i in range(count):
        write(i, tables_ref[pl.ds(base + i, tile_count, stride=8), :])


def first_local(h):
    def body(freq_ref, src_ref, near_in, jac_in, diag_in, flow_ref, weight_ref, near_ref, jac_ref, diag_ref, part_ref, base_ref, map_ref, tables_ref, beside_ref):
        freq = own_freq(freq_ref)

        def write_near(j, rows):
            near_ref[j * 8 : j * 8 + 8, :] = rows

        untile(tables_ref, 0, lambda lanes: near_in[:, lanes].astype(F32), 6, 8, lambda j, rows: write_near(j, rows.astype(jnp.int32)))
        for e in range(5):
            for g in range(5):

                def write_jac(j, rows, e=e, g=g):
                    at = ((j * 5 + e) * 5 + g) * 8
                    jac_ref[at : at + 8, :] = rows

                untile(tables_ref, (6 + e * 5 + g) * 64, lambda lanes, e=e, g=g: jac_in[e, g, :, lanes].astype(F32), 6, 8, write_jac)

            def write_diag(g, rows, e=e):
                at = (e * 5 + g) * 8
                diag_ref[at : at + 8, :] = rows

            untile(tables_ref, (1 + e) * 64, lambda lanes, e=e: diag_in[e, :, lanes], 5, 8, write_diag)
        flow = [load_half(flow_ref, f, h) for f in range(20)]
        for f in range(20):
            store_part(base_ref, f, solve(diag_ref, f // 4, f % 4, flow))
        for q in range(2):
            weight = [None] * 20
            for g in range(5):
                weight[g * 4] = weight_ref[pl.ds(g * 32 + h * 16 + q, 8, stride=2), :]
            for e in range(5):
                row = (e * 2 + q) * 8
                map_ref[row : row + 8, :] = solve(diag_ref, e, 0, weight)
        coupling = local_coupling(h, freq, src_ref, near_ref, jac_ref, beside_ref)
        for f in range(20):
            store_part(part_ref, f, load_part(base_ref, f) - solve(diag_ref, f // 4, f % 4, coupling))

    return body


def wall_terms(freq, wall_of, map_ref):
    w = [wall_of(v) for v in range(8)]
    velocity = [-freq[0] * w[2], -freq[1] * w[3], freq[0] * w[0], freq[1] * w[1]]
    terms = []
    for e in range(5):
        m0 = map_ref[e * 16 : e * 16 + 8, :]
        m1 = map_ref[e * 16 + 8 : e * 16 + 16, :]
        terms += [m0 * velocity[rp] + m1 * w[4 + rp] for rp in range(4)]
    return terms


def last_local(h):
    def body(freq_ref, src_ref, near_ref, jac_ref, diag_ref, base_ref, map_ref, wall_ref, part_ref, beside_ref):
        freq = own_freq(freq_ref)
        terms = wall_terms(freq, lambda v: wall_ref[v * 16 + h * 8 : v * 16 + h * 8 + 8, :], map_ref)
        for f in range(20):
            store_part(part_ref, f, load_part(base_ref, f) + terms[f])
        coupling = local_coupling(h, freq, src_ref, near_ref, jac_ref, beside_ref)
        for f in range(20):
            store_part(part_ref, f, load_part(part_ref, f) - solve(diag_ref, f // 4, f % 4, coupling))

    return body


def ghost_kernel(g0, g1, g2, g3, *refs):
    ghosts = (g0, g1, g2, g3)
    out_ref, beside_ref = refs[8:]
    for h in range(2):
        near_ref, jac_ref, diag_ref, part_ref = refs[h * 4 : h * 4 + 4]
        coupling = couple(
            16, lambda f: [(ghosts[t // 2], f * 2 + t % 2) for t in range(8)], near_ref, jac_ref, beside_ref.at[h]
        )
        for f in range(20):
            store_half(out_ref, f, h, load_part(part_ref, f) - solve(diag_ref, f // 4, f % 4, coupling))


def wall_kernel(freq_ref, recv_ref, send_ref, pre_ref, map0, map1, it_ref, wall_ref, h0, h1, h2, h3, hl_ref):
    freq = own_freq(freq_ref)
    sources = recv_ref.shape[0] // 9
    iota_a = iota_rows(16)
    iota_b = iota_rows(LANES)
    for s in range(sources):
        store_split(hl_ref, s * 16, recv_ref[s * 9 : s * 9 + 8, :])
    total = None
    for c in range(0, sources, CHUNK):
        parts_a, parts_b = [], []
        for s in range(c, c + CHUNK):
            cell = bcast(recv_ref, s * 9 + 8, 16).astype(jnp.int32)
            mask = one_hot(iota_a, narrow(cell >> 7))
            parts_b.append(one_hot(iota_b, narrow(cell & 127)))
            parts_a.append([bcast(hl_ref, s * 16 + v, 16).astype(BF16) * mask for v in range(16)])
        total = add_to(total, parts_a, parts_b)
    wall = total[:LANES] + total[LANES:]
    wall_ref[...] = wall
    for h in range(2):
        terms = wall_terms(freq, lambda v: wall[v * 16 + h * 8 : v * 16 + h * 8 + 8], (map0, map1)[h])
        for f in range(20):
            store_half(it_ref, f, h, load_half(pre_ref, f, h) + terms[f])
    pick_rows(it_ref, send_ref, (h0, h1, h2, h3))


def smem_call(body, operands, outs, scratch=(), specs=None):
    specs = specs or [pl.BlockSpec()] * (len(operands) - 1)
    return pl.pallas_call(
        body,
        grid=(1,),
        out_shape=[jax.ShapeDtypeStruct(shape, dtype) for shape, dtype in outs],
        in_specs=[pl.BlockSpec(memory_space=pltpu.SMEM), *specs],
        scratch_shapes=list(scratch),
        compiler_params=pltpu.CompilerParams(vmem_limit_bytes=56 << 20),
    )(*operands)


def to_rows(field):
    lead = field.shape[:-2]
    inner = field.reshape(*lead, 2, field.shape[-1] // LANES, LANES)
    return jnp.swapaxes(inner, -3, -2).reshape(-1, LANES)


def from_rows(rows, shape):
    inner = rows.reshape(*shape[:-2], shape[-1] // LANES, 2, LANES)
    return jnp.swapaxes(inner, -3, -2).reshape(shape)


ORDER = ((2, 2), (0, 1), (3, -2), (1, -1))


def exchange(blocks):
    ghosts = [None] * 4
    for k, by in ORDER:
        ghosts[k] = from_behind(blocks[k], "dom", by)
    return ghosts


def step(
    spline_blocks,
    modal_coeff,
    frequency,
    face_dest,
    face_cell,
    wall_weight,
    flow_rhs,
    previous,
    diag_inverse,
    off_jacobian,
    neighbor,
    send_list,
):
    dom = lax.axis_size("dom")
    halo = [((40, LANES), F32)] * 4
    part, small, field = ((160, LANES), F32), ((80, LANES), F32), ((320, LANES), F32)
    dest = face_dest.reshape(32, LANES)
    faces = kernel_call(face_kernel, [((4, 8, 1024), F32)])(modal_coeff.transpose(1, 2, 0).reshape(16, 64), spline_blocks)[0]
    faces = lax.all_to_all(faces, "rep", split_axis=0, concat_axis=0, tiled=True)
    slot = kernel_call(slot_kernel, [((32, LANES), jnp.int32)])(dest)[0]
    prev = to_rows(previous)
    rows_out = send_list.reshape(8, LANES)
    picked = kernel_call(pick_kernel, halo)(prev, rows_out)
    ghosts = exchange(picked)
    send = kernel_call(
        dispatch_kernel,
        [((dom * 9, LANES), F32)],
        [pltpu.VMEM((512, LANES), F32)],
    )(faces, dest, slot, face_cell.reshape(32, LANES))[0]
    recv = lax.all_to_all(send.reshape(dom, 9, 1, LANES), "dom", split_axis=0, concat_axis=0, tiled=True)
    recv = recv.reshape(dom * 9, LANES)

    half = neighbor.shape[1] // 2
    jac_in = off_jacobian.transpose(1, 2, 0, 3)
    flow, weight = to_rows(flow_rhs), to_rows(wall_weight)
    beside = pltpu.VMEM((960, LANES), F32)
    tables, parts, bases, maps = [], [], [], []
    for h in range(2):
        specs = [
            pl.BlockSpec(),
            pl.BlockSpec((6, half), lambda i, h=h: (0, h)),
            pl.BlockSpec((5, 5, 6, half), lambda i, h=h: (0, 0, 0, h)),
            pl.BlockSpec((5, 5, half), lambda i, h=h: (0, 0, h)),
            pl.BlockSpec(),
            pl.BlockSpec(),
        ]
        near, jac, diag, p, b, m = smem_call(
            first_local(h),
            (frequency, prev, neighbor, jac_in, diag_inverse, flow, weight),
            [((48, LANES), jnp.int32), ((1200, LANES), F32), ((200, LANES), F32), part, part, small],
            [pltpu.VMEM((31 * 64, LANES), F32), beside],
            specs,
        )
        tables.append((near, jac, diag))
        parts.append(p)
        bases.append(b)
        maps.append(m)
    both_beside = [pltpu.VMEM((2, 960, LANES), F32)]
    pre = kernel_call(ghost_kernel, [field], both_beside)(*ghosts, *tables[0], parts[0], *tables[1], parts[1])[0]
    it, wall, *picked = smem_call(
        wall_kernel,
        (frequency, recv, rows_out, pre, maps[0], maps[1]),
        [field, ((LANES, LANES), F32), *halo],
        [pltpu.VMEM((dom * 16, LANES), F32)],
    )
    ghosts = exchange(picked)
    parts = []
    for h in range(2):
        parts.append(
            smem_call(last_local(h), (frequency, it, *tables[h], bases[h], maps[h], wall), [part], [beside])[0]
        )
    out = kernel_call(ghost_kernel, [field], both_beside)(*ghosts, *tables[0], parts[0], *tables[1], parts[1])[0]
    return from_rows(out, flow_rhs.shape)


def solution(mesh):
    return jax.shard_map(
        step,
        mesh=mesh,
        in_specs=(
            P(("dom", "rep"), None, None, None),
            P(),
            P(),
            P("dom", None),
            P("dom"),
            P(None, None, "dom"),
            P(None, None, "rep", "dom"),
            P(None, None, "rep", "dom"),
            P(None, None, "dom"),
            P(None, None, None, "dom"),
            P(None, "dom"),
            P(None, "dom"),
        ),
        out_specs=P(None, None, "rep", "dom"),
        check_vma=False,
    )
```

time: 86.1 us -> 82.4 us (0.957)
  blocking collectives: 10.7 us -> 0 us
  Pallas kernels: 31.2 us -> 37.4 us
  starting transfers between devices: 31.6 us -> 37.8 us
  local copies, waits for them, and re-layouts: 9.02 us -> 3.74 us
    all_to_all x1 -> x0, blocking collectives: 10.7 us -> none  [shards(): lax.all_to_all(faces, 'rep', split_axis=0, concat_axis=0, tiled=True)]
    pallas_call x6 -> x11, Pallas kernels: 31.2 us -> 37.4 us  [the longest x5 20.2 us: smem_call(): pl.pallas_call(body, grid=(1,), out_shape=[jax.ShapeDtypeStruct(shape, dt...]
    all_to_all x1 -> x2, starting transfers between devices: 10.8 us -> 17 us  [the longest x1 11.5 us: step(): lax.all_to_all(send.reshape(dom, 9, 1, LANES), 'dom', split_axis=0, conca...]
    reshape x6 -> x1, local copies, waits for them, and re-layouts: 5.27 us -> 0.6 us  [step(): rows_out = send_list.reshape(8, LANES)]
    ppermute x8, waiting for transfers between devices: 2.98 us -> 0.02 us  [from_behind(): lax.ppermute(value, axis, [(i, (i + by) % length) for i in range(length)])]
    all_to_all x1 -> x2, waiting for transfers between devices: 0.01 us -> 2.72 us  [the longest x1 2.72 us: step(): lax.all_to_all(faces, 'rep', split_axis=0, concat_axis=0, tiled=True)]
    all_to_all x2 -> x0, local copies, waits for them, and re-layouts: 2.52 us -> none  [shards(): recv = lax.all_to_all(send, 'dom', split_axis=0, concat_axis=0, tiled=True)]
    unnamed x24 -> x22, local copies, waits for them, and re-layouts: 1.22 us -> 3.14 us
  transfers between devices with their start and end apart: 9 -> 10, of which waited for: 2 -> 1; matrix products, arithmetic and copies ran while one was open for 5% -> 1% of each run, Pallas kernels for 13% -> 30%
where the time goes in v2:
time: 82.4 us; the launch traced here: 81.8 us
  starting transfers between devices  37.8 us (46%)
  Pallas kernels  37.4 us (45%)
  local copies, waits for them, and re-layouts  3.74 us (5%)
  waiting for transfers between devices  2.75 us (3%)
    ppermute x8, starting transfers between devices, from_behind(): lax.ppermute(value, axis, [(i, (i + by) % length) for i in range(length)])  20.8 us
    pallas_call x5, Pallas kernels, smem_call(): pl.pallas_call(body, grid=(1,), out_shape=[jax.ShapeDtypeStruct(shape, dt...  20.2 us
    all_to_all x1, starting transfers between devices, step(): lax.all_to_all(send.reshape(dom, 9, 1, LANES), 'dom', split_axis=0, conca...  11.5 us
    pallas_call x2, Pallas kernels, step(): kernel_call(ghost_kernel, [field], both_beside)  8.61 us
    all_to_all x1, starting transfers between devices, step(): lax.all_to_all(faces, 'rep', split_axis=0, concat_axis=0, tiled=True)  5.45 us
    unnamed x22, local copies, waits for them, and re-layouts  3.14 us
    pallas_call x1, Pallas kernels, step(): kernel_call(dispatch_kernel, [((dom * 9, LANES), F32)], [pltpu.VMEM((512,...  3.05 us
    all_to_all x1, waiting for transfers between devices, step(): lax.all_to_all(faces, 'rep', split_axis=0, concat_axis=0, tiled=True)  2.72 us
  transfers between devices with their start and end apart: 10, of which 1 were waited for; matrix products, arithmetic and copies ran while one was open for 1% of the time, Pallas kernels for 30%

profile of v2, /device:TPU:8, one launch (start us, length us, event | category | flops | bytes accessed | tf_op | source)
XLA Modules:
  0.0 81.8 jit_solution(17907868080851028278)
XLA Ops:
  0.0 1.8 %shard_map.118 = f32[4,8,1024]{2,1,0:T(8,128)} custom-call(bf16[16,64]{1,0:T(8,128)(2,1)} %bitcast.42, bf16[8,2,64,128]{3,2,1,0:T(8,128)(2,1)} %spline_ref.1), custom_call_target="tpu_custom_call" | custom-call | tf_op jit(solution)/shard_map/pallas_call | solution.py:380
  1.8 5.4 %all-to-all-start = ((f32[4,8,1024]{2,1,0:T(8,128)}), f32[4,8,1024]{2,1,0:T(8,128)S(1)}, u32[]{:S(2)}, u32[]{:S(2)}) async-start(f32[4,8,1024]{2,1,0:T(8,128)} %shard_map.118), calls=%async_computation | async-start | bytes 262144 | tf_op jit(solution)/shard_map/all_to_all | solution.py:381
  7.3 1.8 %shard_map.119.slot_ref = s32[32,128]{1,0:T(8,128)} custom-call(s32[32,128]{1,0:T(8,128)} %bitcast.39), custom_call_target="tpu_custom_call" | custom-call | tf_op jit(solution)/shard_map/pallas_call | solution.py:382
  9.1 2.7 %all-to-all-done.vals_ref = f32[4,8,1024]{2,1,0:T(8,128)S(1)} async-done(((f32[4,8,1024]{2,1,0:T(8,128)}), f32[4,8,1024]{2,1,0:T(8,128)S(1)}, u32[]{:S(2)}, u32[]{:S(2)}) %all-to-all-start) | async-done | bytes 131104 | tf_op jit(solution)/shard_map/all_to_all | solution.py:381
  11.8 0.0 copy-start.1
  11.8 0.7 copy-done.1
  12.4 3.1 %shard_map.120 = f32[576,128]{1,0:T(8,128)} custom-call(f32[4,8,1024]{2,1,0:T(8,128)} %copy-done.1, s32[32,128]{1,0:T(8,128)} %bitcast.40, s32[32,128]{1,0:T(8,128)} %shard_map.119.slot_ref, s32[32,128]{1,0:T(8,128)} %bitcast.41), custom_call_target="tpu_custom_call" | custom-call | tf_op jit(solution)/shard_map/pallas_call | solution.py:387
  15.5 0.0 copy-start.10
  15.5 11.5 %all-to-all-start.1 = ((f32[64,9,1,128]{3,2,1,0:T(1,128)}), f32[64,9,1,128]{3,2,1,0:T(1,128)S(1)}, u32[]{:S(2)}, u32[]{:S(2)}) async-start(f32[64,9,1,128]{3,2,1,0:T(1,128)} %bitcast.34), calls=%async_computation.1 | async-start | bytes 589824 | tf_op jit(solution)/shard_map/all_to_all | solution.py:392
  27.0 0.0 copy-done.10
  27.0 0.6 reshape.47.send_ref
  27.6 1.9 %shard_map.121 = (f32[40,128]{1,0:T(8,128)}, f32[40,128]{1,0:T(8,128)}, f32[40,128]{1,0:T(8,128)}, f32[40,128]{1,0:T(8,128)}) custom-call(f32[320,128]{1,0:T(8,128)} %bitcast.30, s32[8,128]{1,0:T(8,128)} %reshape.47.send_ref), custom_call_target="tpu_custom_call" | custom-call | tf_op jit(solution)/shard_map/pallas_call | solution.py:385
  29.6 0.1 collective-permute-start
  29.6 5.0 %collective-permute-start.1 = (f32[40,128]{1,0:T(8,128)}, f32[40,128]{1,0:T(8,128)S(1)}, u32[]{:S(2)}, u32[]{:S(2)}) collective-permute-start(f32[40,128]{1,0:T(8,128)} %get-tuple-element.28), channel_id=1, source_target_pairs={{0,252},{4,0},{8,4},{12,8},{16,12},{20,16},{24,20},{28,24},{32,28}... | collective-permute-start | bytes 61448 | tf_op jit(solution)/shard_map/ppermute | solution.py:16
  34.7 0.0 collective-permute-start.2
  34.7 5.3 %collective-permute-start.3 = (f32[40,128]{1,0:T(8,128)}, f32[40,128]{1,0:T(8,128)S(1)}, u32[]{:S(2)}, u32[]{:S(2)}) collective-permute-start(f32[40,128]{1,0:T(8,128)} %get-tuple-element.30), channel_id=1, source_target_pairs={{0,248},{4,252},{8,0},{12,4},{16,8},{20,12},{24,16},{28,20},{32,24... | collective-permute-start | bytes 61448 | tf_op jit(solution)/shard_map/ppermute | solution.py:16
  40.0 4.4 %shard_map.123 = (s32[48,128]{1,0:T(8,128)}, f32[1200,128]{1,0:T(8,128)}, f32[200,128]{1,0:T(8,128)}, f32[160,128]{1,0:T(8,128)}, f32[160,128]{1,0:T(8,128)}, /*index=5*/f32[80,128]{1,0:T(8,128)}) custom-call(f32[8]{0:T(128)} %freq_ref.9, f32[320,128]{1,0:T(8,128)} %bitcast.31, s32[6,2048]{1,0:T(8,128)} %near_in.3, bf16[5,5,6,2048]{3,2,1,0:T(8,128)(2,1)} %bitcast.28, ...), custom_call_target="tpu_custom_call" | custom-call | tf_op jit(solution)/shard_map/pallas_call | solution.py:331
  44.4 4.3 %shard_map.122 = (s32[48,128]{1,0:T(8,128)}, f32[1200,128]{1,0:T(8,128)}, f32[200,128]{1,0:T(8,128)}, f32[160,128]{1,0:T(8,128)}, f32[160,128]{1,0:T(8,128)}, /*index=5*/f32[80,128]{1,0:T(8,128)}) custom-call(f32[8]{0:T(128)} %freq_ref.9, f32[320,128]{1,0:T(8,128)} %bitcast.32, s32[6,2048]{1,0:T(8,128)} %near_in.3, bf16[5,5,6,2048]{3,2,1,0:T(8,128)(2,1)} %bitcast.29, ...), custom_call_target="tpu_custom_call" | custom-call | tf_op jit(solution)/shard_map/pallas_call | solution.py:331
  48.7 0.0 collective-permute-done.g0
  48.7 0.0 copy-start.3
  48.7 0.0 collective-permute-done.1.g1
  48.7 0.0 copy-start.5
  48.8 0.0 collective-permute-done.2.g2
  48.8 0.0 copy-start.7
  48.8 0.0 collective-permute-done.3.g3
  48.8 0.0 copy-start.9
  48.8 0.5 copy-done.3
  49.3 0.0 copy-done.5
  49.4 0.0 copy-done.7
  49.4 0.0 copy-done.9
  49.4 4.3 %shard_map.124.pre_ref = f32[320,128]{1,0:T(8,128)} custom-call(f32[40,128]{1,0:T(8,128)} %copy-done.3, f32[40,128]{1,0:T(8,128)} %copy-done.5, f32[40,128]{1,0:T(8,128)} %copy-done.7, f32[40,128]{1,0:T(8,128)} %copy-done.9, s32[48,128]{1,0:T(8,128)} %get-tuple-element.31.refs_0_.near_ref, f32[1200,128]{1,0:T(8,128)} %get-tuple-element.32.refs_1_.jac_ref, ...), custom_call_target="tpu_custom_call" | custom-call | tf_op jit(solution)/shard_map/pallas_call | solution.py:421
  53.7 0.0 all-to-all-done.1
  53.7 0.0 copy-start
  53.7 0.7 copy-done
  54.4 3.3 %shard_map.125 = (f32[320,128]{1,0:T(8,128)}, f32[128,128]{1,0:T(8,128)}, f32[40,128]{1,0:T(8,128)}, f32[40,128]{1,0:T(8,128)}, f32[40,128]{1,0:T(8,128)}, /*index=5*/f32[40,128]{1,0:T(8,128)}) custom-call(f32[8]{0:T(128)} %freq_ref.9, f32[576,128]{1,0:T(8,128)} %bitcast.33, s32[8,128]{1,0:T(8,128)} %reshape.47.send_ref, f32[320,128]{1,0:T(8,128)} %shard_map.124.pre_ref, ...), custom_call_target="tpu_custom_call" | custom-call | tf_op jit(solution)/shard_map/pallas_call | solution.py:331
  57.7 0.0 collective-permute-start.4
  57.8 5.1 %collective-permute-start.5 = (f32[40,128]{1,0:T(8,128)}, f32[40,128]{1,0:T(8,128)S(1)}, u32[]{:S(2)}, u32[]{:S(2)}) collective-permute-start(f32[40,128]{1,0:T(8,128)} %get-tuple-element.42), channel_id=1, source_target_pairs={{0,252},{4,0},{8,4},{12,8},{16,12},{20,16},{24,20},{28,24},{32,28}... | collective-permute-start | bytes 61448 | tf_op jit(solution)/shard_map/ppermute | solution.py:16
  62.8 0.0 collective-permute-start.6
  62.8 5.3 %collective-permute-start.7 = (f32[40,128]{1,0:T(8,128)}, f32[40,128]{1,0:T(8,128)S(1)}, u32[]{:S(2)}, u32[]{:S(2)}) collective-permute-start(f32[40,128]{1,0:T(8,128)} %get-tuple-element.44), channel_id=1, source_target_pairs={{0,248},{4,252},{8,0},{12,4},{16,8},{20,12},{24,16},{28,20},{32,24... | collective-permute-start | bytes 61448 | tf_op jit(solution)/shard_map/ppermute | solution.py:16
  68.2 4.1 %shard_map.127.refs_7_ = f32[160,128]{1,0:T(8,128)} custom-call(f32[8]{0:T(128)} %freq_ref.9, f32[320,128]{1,0:T(8,128)} %get-tuple-element.45.src_ref, s32[48,128]{1,0:T(8,128)} %get-tuple-element.35.refs_4_.near_ref, f32[1200,128]{1,0:T(8,128)} %get-tuple-element.36.refs_5_.jac_ref, f32[200,128]{1,0:T(8,128)} %get-tuple-element.37.refs_6_.diag_ref, ...), custom_call_target="tpu_custom_call" | custom-call | tf_op jit(solution)/shard_map/pallas_call | solution.py:331
  72.2 4.1 %shard_map.126.refs_3_ = f32[160,128]{1,0:T(8,128)} custom-call(f32[8]{0:T(128)} %freq_ref.9, f32[320,128]{1,0:T(8,128)} %get-tuple-element.45.src_ref, s32[48,128]{1,0:T(8,128)} %get-tuple-element.31.refs_0_.near_ref, f32[1200,128]{1,0:T(8,128)} %get-tuple-element.32.refs_1_.jac_ref, f32[200,128]{1,0:T(8,128)} %get-tuple-element.33.refs_2_.diag_ref, ...), custom_call_target="tpu_custom_call" | custom-call | tf_op jit(solution)/shard_map/pallas_call | solution.py:331
  76.3 0.0 collective-permute-done.4.g0
  76.3 0.0 copy-start.2
  76.3 0.0 collective-permute-done.5.g1
  76.3 0.0 copy-start.4
  76.3 0.0 collective-permute-done.6.g2
  76.3 0.0 copy-start.6
  76.3 0.0 collective-permute-done.7.g3
  76.3 0.5 copy-done.2
  76.9 0.0 copy-done.4
  76.9 0.0 copy-done.6
  76.9 0.0 copy-start.8
  76.9 0.6 copy-done.8
  77.5 4.3 %shard_map.128 = f32[320,128]{1,0:T(8,128)} custom-call(f32[40,128]{1,0:T(8,128)} %copy-done.2, f32[40,128]{1,0:T(8,128)} %copy-done.4, f32[40,128]{1,0:T(8,128)} %copy-done.6, f32[40,128]{1,0:T(8,128)} %copy-done.8, s32[48,128]{1,0:T(8,128)} %get-tuple-element.31.refs_0_.near_ref, f32[1200,128]{1,0:T(8,128)} %get-tuple-element.32.refs_1_.jac_ref, ...), custom_call_target="tpu_custom_call" | custom-call | tf_op jit(solution)/shard_map/pallas_call | solution.py:434
Async XLA Ops:
  1.8 10.0 %all-to-all-start = ((f32[4,8,1024]{2,1,0:T(8,128)}), f32[4,8,1024]{2,1,0:T(8,128)S(1)}, u32[]{:S(2)}, u32[]{:S(2)}) async-start(f32[4,8,1024]{2,1,0:T(8,128)} %shard_map.118), calls=%async_computation | async-start | bytes 262144 | tf_op jit(solution)/shard_map/all_to_all | solution.py:381
  11.8 0.7 copy-start.1
  15.5 11.5 %copy-start.10 = (s32[4,256]{1,0:T(4,128)S(1)}, s32[4,256]{1,0:T(4,128)}, u32[]{:S(2)}) copy-start(s32[4,256]{1,0:T(4,128)} %param.23) | copy-start | bytes 12292
  15.5 38.2 %all-to-all-start.1 = ((f32[64,9,1,128]{3,2,1,0:T(1,128)}), f32[64,9,1,128]{3,2,1,0:T(1,128)S(1)}, u32[]{:S(2)}, u32[]{:S(2)}) async-start(f32[64,9,1,128]{3,2,1,0:T(1,128)} %bitcast.34), calls=%async_computation.1 | async-start | bytes 589824 | tf_op jit(solution)/shard_map/all_to_all | solution.py:392
  29.6 19.1 %collective-permute-start = (f32[40,128]{1,0:T(8,128)}, f32[40,128]{1,0:T(8,128)S(1)}, u32[]{:S(2)}, u32[]{:S(2)}) collective-permute-start(f32[40,128]{1,0:T(8,128)} %get-tuple-element.27), channel_id=1, source_target_pairs={{0,4},{4,8},{8,12},{12,16},{16,20},{20,24},{24,28},{28,32},{32,36}... | collective-permute-start | bytes 61448 | tf_op jit(solution)/shard_map/ppermute | solution.py:16
  29.6 19.1 %collective-permute-start.1 = (f32[40,128]{1,0:T(8,128)}, f32[40,128]{1,0:T(8,128)S(1)}, u32[]{:S(2)}, u32[]{:S(2)}) collective-permute-start(f32[40,128]{1,0:T(8,128)} %get-tuple-element.28), channel_id=1, source_target_pairs={{0,252},{4,0},{8,4},{12,8},{16,12},{20,16},{24,20},{28,24},{32,28}... | collective-permute-start | bytes 61448 | tf_op jit(solution)/shard_map/ppermute | solution.py:16
  34.7 14.1 %collective-permute-start.2 = (f32[40,128]{1,0:T(8,128)}, f32[40,128]{1,0:T(8,128)S(1)}, u32[]{:S(2)}, u32[]{:S(2)}) collective-permute-start(f32[40,128]{1,0:T(8,128)} %get-tuple-element.29), channel_id=1, source_target_pairs={{0,8},{4,12},{8,16},{12,20},{16,24},{20,28},{24,32},{28,36},{32,40... | collective-permute-start | bytes 61448 | tf_op jit(solution)/shard_map/ppermute | solution.py:16
  34.7 14.1 %collective-permute-start.3 = (f32[40,128]{1,0:T(8,128)}, f32[40,128]{1,0:T(8,128)S(1)}, u32[]{:S(2)}, u32[]{:S(2)}) collective-permute-start(f32[40,128]{1,0:T(8,128)} %get-tuple-element.30), channel_id=1, source_target_pairs={{0,248},{4,252},{8,0},{12,4},{16,8},{20,12},{24,16},{28,20},{32,24... | collective-permute-start | bytes 61448 | tf_op jit(solution)/shard_map/ppermute | solution.py:16
  48.7 0.6 copy-start.3
  48.7 0.6 copy-start.5
  48.8 0.6 copy-start.7
  48.8 0.6 copy-start.9
  53.7 0.7 copy-start
  57.7 18.5 %collective-permute-start.4 = (f32[40,128]{1,0:T(8,128)}, f32[40,128]{1,0:T(8,128)S(1)}, u32[]{:S(2)}, u32[]{:S(2)}) collective-permute-start(f32[40,128]{1,0:T(8,128)} %get-tuple-element.41), channel_id=1, source_target_pairs={{0,4},{4,8},{8,12},{12,16},{16,20},{20,24},{24,28},{28,32},{32,36}... | collective-permute-start | bytes 61448 | tf_op jit(solution)/shard_map/ppermute | solution.py:16
  57.8 18.5 %collective-permute-start.5 = (f32[40,128]{1,0:T(8,128)}, f32[40,128]{1,0:T(8,128)S(1)}, u32[]{:S(2)}, u32[]{:S(2)}) collective-permute-start(f32[40,128]{1,0:T(8,128)} %get-tuple-element.42), channel_id=1, source_target_pairs={{0,252},{4,0},{8,4},{12,8},{16,12},{20,16},{24,20},{28,24},{32,28}... | collective-permute-start | bytes 61448 | tf_op jit(solution)/shard_map/ppermute | solution.py:16
  62.8 13.5 %collective-permute-start.6 = (f32[40,128]{1,0:T(8,128)}, f32[40,128]{1,0:T(8,128)S(1)}, u32[]{:S(2)}, u32[]{:S(2)}) collective-permute-start(f32[40,128]{1,0:T(8,128)} %get-tuple-element.43), channel_id=1, source_target_pairs={{0,8},{4,12},{8,16},{12,20},{16,24},{20,28},{24,32},{28,36},{32,40... | collective-permute-start | bytes 61448 | tf_op jit(solution)/shard_map/ppermute | solution.py:16
  62.8 13.5 %collective-permute-start.7 = (f32[40,128]{1,0:T(8,128)}, f32[40,128]{1,0:T(8,128)S(1)}, u32[]{:S(2)}, u32[]{:S(2)}) collective-permute-start(f32[40,128]{1,0:T(8,128)} %get-tuple-element.44), channel_id=1, source_target_pairs={{0,248},{4,252},{8,0},{12,4},{16,8},{20,12},{24,16},{28,20},{32,24... | collective-permute-start | bytes 61448 | tf_op jit(solution)/shard_map/ppermute | solution.py:16
  76.3 0.6 copy-start.2
  76.3 0.6 copy-start.4
  76.3 0.6 copy-start.6
  76.9 0.6 copy-start.8

commit v3 on v2

--- a/solution.py
+++ b/solution.py
@@ -16,13 +16,35 @@
     return lax.ppermute(value, axis, [(i, (i + by) % length) for i in range(length)])
 
 
-def kernel_call(body, outs, scratch=()):
+def call(body, operands, outs, scratch=(), specs=None, smem=0, near_out=()):
+    arrays, in_specs = [], []
+    for place, operand in enumerate(operands):
+        if place < smem:
+            in_specs.append(pl.BlockSpec(memory_space=pltpu.SMEM))
+            arrays.append(operand)
+        elif isinstance(operand, tuple):
+            in_specs.append(pl.BlockSpec(memory_space=pltpu.VMEM))
+            arrays.append(pltpu.with_memory_space_constraint(operand[0], pltpu.VMEM))
+        else:
+            in_specs.append((specs or {}).get(place, pl.BlockSpec()))
+            arrays.append(operand)
+    shapes, out_specs = [], []
+    for place, (shape, dtype) in enumerate(outs):
+        if place in near_out:
+            shapes.append(pltpu.VMEM(shape, dtype))
+            out_specs.append(pl.BlockSpec(memory_space=pltpu.VMEM))
+        else:
+            shapes.append(jax.ShapeDtypeStruct(shape, dtype))
+            out_specs.append(pl.BlockSpec())
     return pl.pallas_call(
         body,
-        out_shape=[jax.ShapeDtypeStruct(shape, dtype) for shape, dtype in outs],
+        grid=(1,),
+        out_shape=shapes,
+        in_specs=in_specs,
+        out_specs=out_specs,
         scratch_shapes=list(scratch),
-        compiler_params=pltpu.CompilerParams(vmem_limit_bytes=56 << 20),
-    )
+        compiler_params=pltpu.CompilerParams(vmem_limit_bytes=24 << 20),
+    )(*arrays)
 
 
 def bcast(ref, row, rows=8):
@@ -326,18 +348,6 @@
     pick_rows(it_ref, send_ref, (h0, h1, h2, h3))
 
 
-def smem_call(body, operands, outs, scratch=(), specs=None):
-    specs = specs or [pl.BlockSpec()] * (len(operands) - 1)
-    return pl.pallas_call(
-        body,
-        grid=(1,),
-        out_shape=[jax.ShapeDtypeStruct(shape, dtype) for shape, dtype in outs],
-        in_specs=[pl.BlockSpec(memory_space=pltpu.SMEM), *specs],
-        scratch_shapes=list(scratch),
-        compiler_params=pltpu.CompilerParams(vmem_limit_bytes=56 << 20),
-    )(*operands)
-
-
 def to_rows(field):
     lead = field.shape[:-2]
     inner = field.reshape(*lead, 2, field.shape[-1] // LANES, LANES)
@@ -349,6 +359,9 @@
     return jnp.swapaxes(inner, -3, -2).reshape(shape)
 
 
+NEAR_FACE = (0,)
+NEAR_PICK = range(4)
+NEAR_SEND = (0,)
 ORDER = ((2, 2), (0, 1), (3, -2), (1, -1))
 
 
@@ -377,18 +390,21 @@
     halo = [((40, LANES), F32)] * 4
     part, small, field = ((160, LANES), F32), ((80, LANES), F32), ((320, LANES), F32)
     dest = face_dest.reshape(32, LANES)
-    faces = kernel_call(face_kernel, [((4, 8, 1024), F32)])(modal_coeff.transpose(1, 2, 0).reshape(16, 64), spline_blocks)[0]
+    coef = modal_coeff.transpose(1, 2, 0).reshape(16, 64)
+    faces = call(face_kernel, (coef, spline_blocks), [((4, 8, 1024), F32)], near_out=NEAR_FACE)[0]
     faces = lax.all_to_all(faces, "rep", split_axis=0, concat_axis=0, tiled=True)
-    slot = kernel_call(slot_kernel, [((32, LANES), jnp.int32)])(dest)[0]
+    slot = call(slot_kernel, (dest,), [((32, LANES), jnp.int32)], near_out=(0,))[0]
     prev = to_rows(previous)
     rows_out = send_list.reshape(8, LANES)
-    picked = kernel_call(pick_kernel, halo)(prev, rows_out)
+    picked = call(pick_kernel, (prev, rows_out), halo, near_out=NEAR_PICK)
     ghosts = exchange(picked)
-    send = kernel_call(
+    send = call(
         dispatch_kernel,
+        ((faces,), dest, (slot,), face_cell.reshape(32, LANES)),
         [((dom * 9, LANES), F32)],
         [pltpu.VMEM((512, LANES), F32)],
-    )(faces, dest, slot, face_cell.reshape(32, LANES))[0]
+        near_out=NEAR_SEND,
+    )[0]
     recv = lax.all_to_all(send.reshape(dom, 9, 1, LANES), "dom", split_axis=0, concat_axis=0, tiled=True)
     recv = recv.reshape(dom * 9, LANES)
 
@@ -398,40 +414,53 @@
     beside = pltpu.VMEM((960, LANES), F32)
     tables, parts, bases, maps = [], [], [], []
     for h in range(2):
-        specs = [
-            pl.BlockSpec(),
-            pl.BlockSpec((6, half), lambda i, h=h: (0, h)),
-            pl.BlockSpec((5, 5, 6, half), lambda i, h=h: (0, 0, 0, h)),
-            pl.BlockSpec((5, 5, half), lambda i, h=h: (0, 0, h)),
-            pl.BlockSpec(),
-            pl.BlockSpec(),
-        ]
-        near, jac, diag, p, b, m = smem_call(
+        specs = {
+            2: pl.BlockSpec((6, half), lambda i, h=h: (0, h)),
+            3: pl.BlockSpec((5, 5, 6, half), lambda i, h=h: (0, 0, 0, h)),
+            4: pl.BlockSpec((5, 5, half), lambda i, h=h: (0, 0, h)),
+        }
+        near, jac, diag, p, b, m = call(
             first_local(h),
             (frequency, prev, neighbor, jac_in, diag_inverse, flow, weight),
             [((48, LANES), jnp.int32), ((1200, LANES), F32), ((200, LANES), F32), part, part, small],
             [pltpu.VMEM((31 * 64, LANES), F32), beside],
             specs,
+            smem=1,
+            near_out=range(6),
         )
-        tables.append((near, jac, diag))
-        parts.append(p)
-        bases.append(b)
-        maps.append(m)
+        tables += [(near,), (jac,), (diag,)]
+        parts.append((p,))
+        bases.append((b,))
+        maps.append((m,))
     both_beside = [pltpu.VMEM((2, 960, LANES), F32)]
-    pre = kernel_call(ghost_kernel, [field], both_beside)(*ghosts, *tables[0], parts[0], *tables[1], parts[1])[0]
-    it, wall, *picked = smem_call(
+
+    def ghost_part(ghosts, parts, near_out):
+        operands = (*[(g,) for g in ghosts], *tables[:3], parts[0], *tables[3:], parts[1])
+        return call(ghost_kernel, operands, [field], both_beside, near_out=near_out)[0]
+
+    pre = ghost_part(ghosts, parts, (0,))
+    it, wall, *picked = call(
         wall_kernel,
-        (frequency, recv, rows_out, pre, maps[0], maps[1]),
+        (frequency, (recv,), (rows_out,), (pre,), *maps),
         [field, ((LANES, LANES), F32), *halo],
         [pltpu.VMEM((dom * 16, LANES), F32)],
+        smem=1,
+        near_out=range(6),
     )
     ghosts = exchange(picked)
     parts = []
     for h in range(2):
         parts.append(
-            smem_call(last_local(h), (frequency, it, *tables[h], bases[h], maps[h], wall), [part], [beside])[0]
+            call(
+                last_local(h),
+                (frequency, (it,), *tables[3 * h : 3 * h + 3], bases[h], maps[h], (wall,)),
+                [part],
+                [beside],
+                smem=1,
+                near_out=(0,),
+            )
         )
-    out = kernel_call(ghost_kernel, [field], both_beside)(*ghosts, *tables[0], parts[0], *tables[1], parts[1])[0]
+    out = ghost_part(ghosts, [tuple(p) for p in parts], ())
     return from_rows(out, flow_rhs.shape)
 
 

time: 82.4 us -> 68.8 us (0.83)
  Pallas kernels: 37.4 us -> 22.6 us
  waiting for transfers between devices: 2.75 us -> 4.03 us
    pallas_call x11, Pallas kernels: 37.4 us -> 22.6 us  [call(): pl.pallas_call(body, grid=(1,), out_shape=shapes, in_specs=in_specs, out_...]
    all_to_all x1, waiting for transfers between devices: 2.72 us -> 4.01 us  [step(): lax.all_to_all(faces, 'rep', split_axis=0, concat_axis=0, tiled=True)]
    unnamed x22 -> x32, local copies, waits for them, and re-layouts: 3.14 us -> 3.56 us
  transfers between devices with their start and end apart: 10 -> 10, of which waited for: 1 -> 1; matrix products, arithmetic and copies ran while one was open for 1% -> 0% of each run, Pallas kernels for 30% -> 21%
where the time goes in v3:
time: 68.8 us; the launch traced here: 68.5 us
  starting transfers between devices  38.1 us (55%)
  Pallas kernels  22.6 us (33%)
  waiting for transfers between devices  4.03 us (6%)
  local copies, waits for them, and re-layouts  3.57 us (5%)
    pallas_call x11, Pallas kernels, call(): pl.pallas_call(body, grid=(1,), out_shape=shapes, in_specs=in_specs, out_...  22.6 us
    ppermute x8, starting transfers between devices, from_behind(): lax.ppermute(value, axis, [(i, (i + by) % length) for i in range(length)])  21 us
    all_to_all x1, starting transfers between devices, step(): lax.all_to_all(send.reshape(dom, 9, 1, LANES), 'dom', split_axis=0, conca...  11.5 us
    all_to_all x1, starting transfers between devices, step(): lax.all_to_all(faces, 'rep', split_axis=0, concat_axis=0, tiled=True)  5.58 us
    all_to_all x1, waiting for transfers between devices, step(): lax.all_to_all(faces, 'rep', split_axis=0, concat_axis=0, tiled=True)  4.01 us
    unnamed x32, local copies, waits for them, and re-layouts  3.56 us
  transfers between devices with their start and end apart: 10, of which 1 were waited for; matrix products, arithmetic and copies ran while one was open for 0% of the time, Pallas kernels for 21%

profile of v3, /device:TPU:8, one launch (start us, length us, event | category | flops | bytes accessed | tf_op | source)
XLA Modules:
  0.0 68.5 jit_solution(11126628432568248049)
XLA Ops:
  0.0 0.0 copy-start.6
  0.0 0.9 %copy-done.6 = bf16[8,2,64,128]{3,2,1,0:T(8,128)(2,1)S(1)} copy-done((bf16[8,2,64,128]{3,2,1,0:T(8,128)(2,1)S(1)}, bf16[8,2,64,128]{3,2,1,0:T(8,128)(2,1)}, u32[]{:S(2)}) %copy-start.6) | copy-done | bytes 262168
  1.0 0.0 copy-start.14
  1.0 0.7 %copy-done.14 = bf16[64,2,8]{0,2,1:T(8,128)(2,1)S(1)} copy-done((bf16[64,2,8]{0,2,1:T(8,128)(2,1)S(1)}, bf16[64,2,8]{0,2,1:T(8,128)(2,1)}, u32[]{:S(2)}) %copy-start.14) | copy-done | bytes 2072
  1.6 0.0 copy-start.11
  1.6 0.0 copy-start.12
  1.6 0.0 copy-start.15
  1.6 0.0 copy-start.5
  1.6 0.8 %shard_map.118 = f32[4,8,1024]{2,1,0:T(8,128)} custom-call(bf16[16,64]{1,0:T(8,128)(2,1)S(1)} %bitcast.41, bf16[8,2,64,128]{3,2,1,0:T(8,128)(2,1)S(1)} %copy-done.6), custom_call_target="tpu_custom_call" | custom-call | tf_op jit(solution)/shard_map/pallas_call | solution.py:39
  2.5 0.0 copy-start
  2.5 5.6 %all-to-all-start = ((f32[4,8,1024]{2,1,0:T(8,128)}), f32[4,8,1024]{2,1,0:T(8,128)S(1)}, u32[]{:S(2)}, u32[]{:S(2)}) async-start(f32[4,8,1024]{2,1,0:T(8,128)} %shard_map.118), calls=%async_computation | async-start | bytes 262144 | tf_op jit(solution)/shard_map/all_to_all | solution.py:395
  8.1 0.0 copy-done.11
  8.1 0.5 shard_map.119.slot_ref
  8.6 4.0 %all-to-all-done.vals_ref = f32[4,8,1024]{2,1,0:T(8,128)S(1)} async-done(((f32[4,8,1024]{2,1,0:T(8,128)}), f32[4,8,1024]{2,1,0:T(8,128)S(1)}, u32[]{:S(2)}, u32[]{:S(2)}) %all-to-all-start) | async-done | bytes 131104 | tf_op jit(solution)/shard_map/all_to_all | solution.py:395
  12.6 0.0 copy-done.12
  12.6 2.1 %shard_map.120 = f32[576,128]{1,0:T(8,128)} custom-call(f32[4,8,1024]{2,1,0:T(8,128)S(1)} %all-to-all-done.vals_ref, s32[32,128]{1,0:T(8,128)S(1)} %bitcast.39, s32[32,128]{1,0:T(8,128)S(1)} %shard_map.119.slot_ref, s32[32,128]{1,0:T(8,128)S(1)} %bitcast.40), custom_call_target="tpu_custom_call" | custom-call | tf_op jit(solution)/shard_map/pallas_call | solution.py:39
  14.7 0.0 copy-start.1
  14.7 0.0 copy-start.2
  14.8 0.0 copy-start.4
  14.8 11.5 %all-to-all-start.1 = ((f32[64,9,1,128]{3,2,1,0:T(1,128)}), f32[64,9,1,128]{3,2,1,0:T(1,128)S(1)}, u32[]{:S(2)}, u32[]{:S(2)}) async-start(f32[64,9,1,128]{3,2,1,0:T(1,128)} %bitcast.4), calls=%async_computation.1 | async-start | bytes 589824 | tf_op jit(solution)/shard_map/all_to_all | solution.py:408
  26.3 0.0 copy-done.15
  26.3 0.0 copy-start.3
  26.3 0.0 copy-done.1
  26.3 0.4 shard_map.121
  26.7 0.1 collective-permute-start
  26.9 5.0 %collective-permute-start.1 = (f32[40,128]{1,0:T(8,128)S(1)}, f32[40,128]{1,0:T(8,128)S(1)}, u32[]{:S(2)}, u32[]{:S(2)}) collective-permute-start(f32[40,128]{1,0:T(8,128)S(1)} %get-tuple-element.28), channel_id=1, source_target_pairs={{0,252},{4,0},{8,4},{12,8},{16,12},{20,16},{24,20},{28,24},{32,28}... | collective-permute-start | bytes 61448 | tf_op jit(solution)/shard_map/ppermute | solution.py:16
  31.9 0.0 collective-permute-start.2
  31.9 5.3 %collective-permute-start.3 = (f32[40,128]{1,0:T(8,128)S(1)}, f32[40,128]{1,0:T(8,128)S(1)}, u32[]{:S(2)}, u32[]{:S(2)}) collective-permute-start(f32[40,128]{1,0:T(8,128)S(1)} %get-tuple-element.30), channel_id=1, source_target_pairs={{0,248},{4,252},{8,0},{12,4},{16,8},{20,12},{24,16},{28,20},{32,24... | collective-permute-start | bytes 61448 | tf_op jit(solution)/shard_map/ppermute | solution.py:16
  37.2 0.0 copy-start.13
  37.2 0.0 copy-done.5
  37.2 0.0 copy-done
  37.2 0.0 copy-done.2
  37.2 0.0 copy-done.4
  37.2 0.0 copy-done.3
  37.3 0.6 copy-done.13
  37.9 2.8 %shard_map.123 = (s32[48,128]{1,0:T(8,128)S(1)}, f32[1200,128]{1,0:T(8,128)S(1)}, f32[200,128]{1,0:T(8,128)S(1)}, f32[160,128]{1,0:T(8,128)S(1)}, f32[160,128]{1,0:T(8,128)S(1)}, /*index=5*/f32[80,128]{1,0:T(8,128)S(1)}) custom-call(f32[8]{0:T(128)S(1)} %copy-done.13, f32[320,128]{1,0:T(8,128)S(1)} %bitcast.31, s32[6,2048]{1,0:T(8,128)S(1)} %copy-done.5, ...), custom_call_target="tpu_custom_call" | custom-call | tf_op jit(solution)/shard_map/pallas_call | solution.py:39
  40.7 0.0 copy-start.7
  40.7 0.6 copy-done.7
  41.3 2.8 %shard_map.122 = (s32[48,128]{1,0:T(8,128)S(1)}, f32[1200,128]{1,0:T(8,128)S(1)}, f32[200,128]{1,0:T(8,128)S(1)}, f32[160,128]{1,0:T(8,128)S(1)}, f32[160,128]{1,0:T(8,128)S(1)}, /*index=5*/f32[80,128]{1,0:T(8,128)S(1)}) custom-call(f32[8]{0:T(128)S(1)} %copy-done.13, f32[320,128]{1,0:T(8,128)S(1)} %bitcast.32, s32[6,2048]{1,0:T(8,128)S(1)} %copy-done.5, ...), custom_call_target="tpu_custom_call" | custom-call | tf_op jit(solution)/shard_map/pallas_call | solution.py:39
  44.1 0.0 copy-start.9
  44.2 0.6 copy-done.9
  44.8 0.0 collective-permute-done.g0
  44.8 0.0 collective-permute-done.1.g1
  44.8 0.0 collective-permute-done.2.g2
  44.8 0.0 collective-permute-done.3.g3
  44.8 2.2 %shard_map.124.pre_ref = f32[320,128]{1,0:T(8,128)S(1)} custom-call(f32[40,128]{1,0:T(8,128)S(1)} %collective-permute-done.g0, f32[40,128]{1,0:T(8,128)S(1)} %collective-permute-done.1.g1, f32[40,128]{1,0:T(8,128)S(1)} %collective-permute-done.2.g2, f32[40,128]{1,0:T(8,128)S(1)} %collective-permute-done.3.g3, ...), custom_call_target="tpu_custom_call" | custom-call | tf_op jit(solution)/shard_map/pallas_call | solution.py:39
  47.0 0.0 all-to-all-done.1
  47.1 0.0 copy-start.8
  47.1 2.2 %shard_map.125 = (f32[320,128]{1,0:T(8,128)S(1)}, f32[128,128]{1,0:T(8,128)S(1)}, f32[40,128]{1,0:T(8,128)S(1)}, f32[40,128]{1,0:T(8,128)S(1)}, f32[40,128]{1,0:T(8,128)S(1)}, /*index=5*/f32[40,128]{1,0:T(8,128)S(1)}) custom-call(f32[8]{0:T(128)S(1)} %copy-done.13, f32[576,128]{1,0:T(8,128)S(1)} %bitcast.33, s32[8,128]{1,0:T(8,128)S(1)} %reshape.47.send_ref, ...), custom_call_target="tpu_custom_call" | custom-call | tf_op jit(solution)/shard_map/pallas_call | solution.py:39
  49.3 0.1 collective-permute-start.4
  49.4 5.1 %collective-permute-start.5 = (f32[40,128]{1,0:T(8,128)S(1)}, f32[40,128]{1,0:T(8,128)S(1)}, u32[]{:S(2)}, u32[]{:S(2)}) collective-permute-start(f32[40,128]{1,0:T(8,128)S(1)} %get-tuple-element.42), channel_id=1, source_target_pairs={{0,252},{4,0},{8,4},{12,8},{16,12},{20,16},{24,20},{28,24},{32,28}... | collective-permute-start | bytes 61448 | tf_op jit(solution)/shard_map/ppermute | solution.py:16
  54.4 0.0 collective-permute-start.6
  54.4 5.3 %collective-permute-start.7 = (f32[40,128]{1,0:T(8,128)S(1)}, f32[40,128]{1,0:T(8,128)S(1)}, u32[]{:S(2)}, u32[]{:S(2)}) collective-permute-start(f32[40,128]{1,0:T(8,128)S(1)} %get-tuple-element.44), channel_id=1, source_target_pairs={{0,248},{4,252},{8,0},{12,4},{16,8},{20,12},{24,16},{28,20},{32,24... | collective-permute-start | bytes 61448 | tf_op jit(solution)/shard_map/ppermute | solution.py:16
  59.8 0.0 copy-done.8
  59.8 0.0 copy-start.10
  59.8 2.8 %shard_map.127.refs_7_ = f32[160,128]{1,0:T(8,128)S(1)} custom-call(f32[8]{0:T(128)S(1)} %copy-done.13, f32[320,128]{1,0:T(8,128)S(1)} %get-tuple-element.45.src_ref, s32[48,128]{1,0:T(8,128)S(1)} %get-tuple-element.35.refs_4_.near_ref, f32[1200,128]{1,0:T(8,128)S(1)} %get-tuple-element.36.refs_5_.jac_ref, ...), custom_call_target="tpu_custom_call" | custom-call | tf_op jit(solution)/shard_map/pallas_call | solution.py:39
  62.6 0.0 copy-done.10
  62.6 2.8 %shard_map.126.refs_3_ = f32[160,128]{1,0:T(8,128)S(1)} custom-call(f32[8]{0:T(128)S(1)} %copy-done.13, f32[320,128]{1,0:T(8,128)S(1)} %get-tuple-element.45.src_ref, s32[48,128]{1,0:T(8,128)S(1)} %get-tuple-element.31.refs_0_.near_ref, f32[1200,128]{1,0:T(8,128)S(1)} %get-tuple-element.32.refs_1_.jac_ref, ...), custom_call_target="tpu_custom_call" | custom-call | tf_op jit(solution)/shard_map/pallas_call | solution.py:39
  65.5 0.0 collective-permute-done.4.g0
  65.5 0.0 collective-permute-done.5.g1
  65.5 0.0 collective-permute-done.6.g2
  65.5 0.0 collective-permute-done.7.g3
  65.5 3.0 %shard_map.128 = f32[320,128]{1,0:T(8,128)} custom-call(f32[40,128]{1,0:T(8,128)S(1)} %collective-permute-done.4.g0, f32[40,128]{1,0:T(8,128)S(1)} %collective-permute-done.5.g1, f32[40,128]{1,0:T(8,128)S(1)} %collective-permute-done.6.g2, f32[40,128]{1,0:T(8,128)S(1)} %collective-permute-done.7.g3, s32[48,128]{1,0:T(8,128)S(1)} %get-tuple-element.31.refs_0_.near_ref, ...), custom_call_target="tpu_custom_call" | custom-call | tf_op jit(solution)/shard_map/pallas_call | solution.py:39
  (1 shorter events, 0.0 us)
Async XLA Ops:
  0.0 0.9 %copy-start.6 = (bf16[8,2,64,128]{3,2,1,0:T(8,128)(2,1)S(1)}, bf16[8,2,64,128]{3,2,1,0:T(8,128)(2,1)}, u32[]{:S(2)}) copy-start(bf16[8,2,64,128]{3,2,1,0:T(8,128)(2,1)} %spline_ref.1) | copy-start | bytes 786436
  1.0 0.7 %copy-start.14 = (bf16[64,2,8]{0,2,1:T(8,128)(2,1)S(1)}, bf16[64,2,8]{0,2,1:T(8,128)(2,1)}, u32[]{:S(2)}) copy-start(bf16[64,2,8]{0,2,1:T(8,128)(2,1)} %param.13) | copy-start | bytes 6148
  1.6 6.4 %copy-start.11 = (s32[4096,1]{0,1:T(1,128)S(1)}, s32[4096,1]{0,1:T(1,128)}, u32[]{:S(2)}) copy-start(s32[4096,1]{0,1:T(1,128)} %param.15) | copy-start | bytes 49156
  1.6 11.0 %copy-start.12 = (s32[4096]{0:T(1024)S(1)}, s32[4096]{0:T(1024)}, u32[]{:S(2)}) copy-start(s32[4096]{0:T(1024)} %param.16) | copy-start | bytes 49156
  1.6 24.6 %copy-start.15 = (s32[4,256]{1,0:T(4,128)S(1)}, s32[4,256]{1,0:T(4,128)}, u32[]{:S(2)}) copy-start(s32[4,256]{1,0:T(4,128)} %param.23) | copy-start | bytes 12292
  1.6 35.6 %copy-start.5 = (s32[6,2048]{1,0:T(8,128)S(1)}, s32[6,2048]{1,0:T(8,128)}, u32[]{:S(2)}) copy-start(s32[6,2048]{1,0:T(8,128)} %near_in.3) | copy-start | bytes 147460
  2.5 34.7 %copy-start = (bf16[6,5,5,2048]{3,0,2,1:T(8,128)(2,1)S(1)}, bf16[6,5,5,2048]{3,0,2,1:T(8,128)(2,1)}, u32[]{:S(2)}) copy-start(bf16[6,5,5,2048]{3,0,2,1:T(8,128)(2,1)} %param.21) | copy-start | bytes 1843204
  2.5 10.1 %all-to-all-start = ((f32[4,8,1024]{2,1,0:T(8,128)}), f32[4,8,1024]{2,1,0:T(8,128)S(1)}, u32[]{:S(2)}, u32[]{:S(2)}) async-start(f32[4,8,1024]{2,1,0:T(8,128)} %shard_map.118), calls=%async_computation | async-start | bytes 262144 | tf_op jit(solution)/shard_map/all_to_all | solution.py:395
  14.7 11.6 %copy-start.1 = (f32[5,2,2,2048]{3,2,1,0:T(2,128)S(1)}, f32[5,2,2,2048]{3,2,1,0:T(2,128)}, u32[]{:S(2)}) copy-start(f32[5,2,2,2048]{3,2,1,0:T(2,128)} %param.19) | copy-start | bytes 491524
  14.7 22.5 %copy-start.2 = (f32[5,5,2048]{2,1,0:T(8,128)S(1)}, f32[5,5,2048]{2,1,0:T(8,128)}, u32[]{:S(2)}) copy-start(f32[5,5,2048]{2,1,0:T(8,128)} %diag_in.3) | copy-start | bytes 614404
  14.8 22.5 %copy-start.4 = (f32[5,2,2048]{2,1,0:T(2,128)S(1)}, f32[5,2,2048]{2,1,0:T(2,128)}, u32[]{:S(2)}) copy-start(f32[5,2,2048]{2,1,0:T(2,128)} %param.17) | copy-start | bytes 245764
  14.8 32.3 %all-to-all-start.1 = ((f32[64,9,1,128]{3,2,1,0:T(1,128)}), f32[64,9,1,128]{3,2,1,0:T(1,128)S(1)}, u32[]{:S(2)}, u32[]{:S(2)}) async-start(f32[64,9,1,128]{3,2,1,0:T(1,128)} %bitcast.4), calls=%async_computation.1 | async-start | bytes 589824 | tf_op jit(solution)/shard_map/all_to_all | solution.py:408
  26.3 11.0 %copy-start.3 = (f32[5,2,2,2048]{3,2,1,0:T(2,128)S(1)}, f32[5,2,2,2048]{3,2,1,0:T(2,128)}, u32[]{:S(2)}) copy-start(f32[5,2,2,2048]{3,2,1,0:T(2,128)} %param.18) | copy-start | bytes 491524
  26.7 18.1 %collective-permute-start = (f32[40,128]{1,0:T(8,128)S(1)}, f32[40,128]{1,0:T(8,128)S(1)}, u32[]{:S(2)}, u32[]{:S(2)}) collective-permute-start(f32[40,128]{1,0:T(8,128)S(1)} %get-tuple-element.27), channel_id=1, source_target_pairs={{0,4},{4,8},{8,12},{12,16},{16,20},{20,24},{24,28},{28,32},{32,36}... | collective-permute-start | bytes 61448 | tf_op jit(solution)/shard_map/ppermute | solution.py:16
  26.9 17.9 %collective-permute-start.1 = (f32[40,128]{1,0:T(8,128)S(1)}, f32[40,128]{1,0:T(8,128)S(1)}, u32[]{:S(2)}, u32[]{:S(2)}) collective-permute-start(f32[40,128]{1,0:T(8,128)S(1)} %get-tuple-element.28), channel_id=1, source_target_pairs={{0,252},{4,0},{8,4},{12,8},{16,12},{20,16},{24,20},{28,24},{32,28}... | collective-permute-start | bytes 61448 | tf_op jit(solution)/shard_map/ppermute | solution.py:16
  31.9 12.9 %collective-permute-start.2 = (f32[40,128]{1,0:T(8,128)S(1)}, f32[40,128]{1,0:T(8,128)S(1)}, u32[]{:S(2)}, u32[]{:S(2)}) collective-permute-start(f32[40,128]{1,0:T(8,128)S(1)} %get-tuple-element.29), channel_id=1, source_target_pairs={{0,8},{4,12},{8,16},{12,20},{16,24},{20,28},{24,32},{28,36},{32,40... | collective-permute-start | bytes 61448 | tf_op jit(solution)/shard_map/ppermute | solution.py:16
  31.9 12.9 %collective-permute-start.3 = (f32[40,128]{1,0:T(8,128)S(1)}, f32[40,128]{1,0:T(8,128)S(1)}, u32[]{:S(2)}, u32[]{:S(2)}) collective-permute-start(f32[40,128]{1,0:T(8,128)S(1)} %get-tuple-element.30), channel_id=1, source_target_pairs={{0,248},{4,252},{8,0},{12,4},{16,8},{20,12},{24,16},{28,20},{32,24... | collective-permute-start | bytes 61448 | tf_op jit(solution)/shard_map/ppermute | solution.py:16
  37.2 0.7 copy-start.13
  40.7 0.6 copy-start.7
  44.1 0.6 copy-start.9
  47.1 12.7 %copy-start.8 = (f32[160,128]{1,0:T(8,128)S(1)}, f32[160,128]{1,0:T(8,128)}, u32[]{:S(2)}) copy-start(f32[160,128]{1,0:T(8,128)} %copy-done.7) | copy-start | bytes 245764
  49.3 16.2 %collective-permute-start.4 = (f32[40,128]{1,0:T(8,128)S(1)}, f32[40,128]{1,0:T(8,128)S(1)}, u32[]{:S(2)}, u32[]{:S(2)}) collective-permute-start(f32[40,128]{1,0:T(8,128)S(1)} %get-tuple-element.41), channel_id=1, source_target_pairs={{0,4},{4,8},{8,12},{12,16},{16,20},{20,24},{24,28},{28,32},{32,36}... | collective-permute-start | bytes 61448 | tf_op jit(solution)/shard_map/ppermute | solution.py:16
  49.4 16.1 %collective-permute-start.5 = (f32[40,128]{1,0:T(8,128)S(1)}, f32[40,128]{1,0:T(8,128)S(1)}, u32[]{:S(2)}, u32[]{:S(2)}) collective-permute-start(f32[40,128]{1,0:T(8,128)S(1)} %get-tuple-element.42), channel_id=1, source_target_pairs={{0,252},{4,0},{8,4},{12,8},{16,12},{20,16},{24,20},{28,24},{32,28}... | collective-permute-start | bytes 61448 | tf_op jit(solution)/shard_map/ppermute | solution.py:16
  54.4 11.1 %collective-permute-start.6 = (f32[40,128]{1,0:T(8,128)S(1)}, f32[40,128]{1,0:T(8,128)S(1)}, u32[]{:S(2)}, u32[]{:S(2)}) collective-permute-start(f32[40,128]{1,0:T(8,128)S(1)} %get-tuple-element.43), channel_id=1, source_target_pairs={{0,8},{4,12},{8,16},{12,20},{16,24},{20,28},{24,32},{28,36},{32,40... | collective-permute-start | bytes 61448 | tf_op jit(solution)/shard_map/ppermute | solution.py:16
  54.4 11.1 %collective-permute-start.7 = (f32[40,128]{1,0:T(8,128)S(1)}, f32[40,128]{1,0:T(8,128)S(1)}, u32[]{:S(2)}, u32[]{:S(2)}) collective-permute-start(f32[40,128]{1,0:T(8,128)S(1)} %get-tuple-element.44), channel_id=1, source_target_pairs={{0,248},{4,252},{8,0},{12,4},{16,8},{20,12},{24,16},{28,20},{32,24... | collective-permute-start | bytes 61448 | tf_op jit(solution)/shard_map/ppermute | solution.py:16
  59.8 2.8 %copy-start.10 = (f32[160,128]{1,0:T(8,128)S(1)}, f32[160,128]{1,0:T(8,128)}, u32[]{:S(2)}) copy-start(f32[160,128]{1,0:T(8,128)} %copy-done.9) | copy-start | bytes 245764

commit v4 on v3

--- a/solution.py
+++ b/solution.py
@@ -79,9 +79,12 @@
     return jnp.where(iota == full, jnp.ones_like(iota), jnp.zeros_like(iota))
 
 
-def slot_kernel(dest_ref, slot_ref):
+def slot_kernel(freq_ref, dest_ref, slot_ref, plane_ref):
     doms = 64
     tiles = dest_ref.shape[0]
+    first = lax.axis_index("rep") * 2
+    for p in range(2):
+        plane_ref[p * 8 : p * 8 + 8, :] = jnp.full((8, LANES), freq_ref[first + p], F32)
     iota_d = lax.broadcasted_iota(jnp.int32, (doms, LANES), 0)
     iota_p = lax.broadcasted_iota(jnp.int32, (LANES, LANES), 0)
     iota_l = lax.broadcasted_iota(jnp.int32, (LANES, LANES), 1)
@@ -227,9 +230,8 @@
     return coupling
 
 
-def own_freq(freq_ref):
-    first = lax.axis_index("rep") * 2
-    return [freq_ref[first], freq_ref[first + 1]]
+def own_freq(plane_ref):
+    return [plane_ref[0:8, :], plane_ref[8:16, :]]
 
 
 def solve(diag_ref, e, rp, parts):
@@ -248,31 +250,36 @@
         write(i, tables_ref[pl.ds(base + i, tile_count, stride=8), :])
 
 
-def first_local(h):
-    def body(freq_ref, src_ref, near_in, jac_in, diag_in, flow_ref, weight_ref, near_ref, jac_ref, diag_ref, part_ref, base_ref, map_ref, tables_ref, beside_ref):
-        freq = own_freq(freq_ref)
-
-        def write_near(j, rows):
-            near_ref[j * 8 : j * 8 + 8, :] = rows
-
-        untile(tables_ref, 0, lambda lanes: near_in[:, lanes].astype(F32), 6, 8, lambda j, rows: write_near(j, rows.astype(jnp.int32)))
+def first_kernel(freq_ref, src_ref, near_in, jac_in, diag_in, flow_ref, weight_ref, *refs):
+    freq = own_freq(freq_ref)
+    scratch_ref, beside_ref = refs[10:]
+    for h in range(2):
+        near_ref, jac_ref, diag_ref, map_ref, part_ref = refs[h * 5 : h * 5 + 5]
+        tables_ref = scratch_ref.at[h]
+        start = h * near_ref.shape[0] // 6 * LANES
+
+        def cells(lanes, start=start):
+            return slice(start + lanes.start, start + lanes.stop)
+
+        def write_near(j, rows, near_ref=near_ref):
+            near_ref[j * 8 : j * 8 + 8, :] = rows.astype(jnp.int32)
+
+        untile(tables_ref, 0, lambda lanes: near_in[:, cells(lanes)].astype(F32), 6, 8, write_near)
         for e in range(5):
             for g in range(5):
 
-                def write_jac(j, rows, e=e, g=g):
+                def write_jac(j, rows, e=e, g=g, jac_ref=jac_ref):
                     at = ((j * 5 + e) * 5 + g) * 8
                     jac_ref[at : at + 8, :] = rows
 
-                untile(tables_ref, (6 + e * 5 + g) * 64, lambda lanes, e=e, g=g: jac_in[e, g, :, lanes].astype(F32), 6, 8, write_jac)
-
-            def write_diag(g, rows, e=e):
+                at = (6 + e * 5 + g) * 64
+                untile(tables_ref, at, lambda lanes, e=e, g=g: jac_in[e, g, :, cells(lanes)].astype(F32), 6, 8, write_jac)
+
+            def write_diag(g, rows, e=e, diag_ref=diag_ref):
                 at = (e * 5 + g) * 8
                 diag_ref[at : at + 8, :] = rows
 
-            untile(tables_ref, (1 + e) * 64, lambda lanes, e=e: diag_in[e, :, lanes], 5, 8, write_diag)
-        flow = [load_half(flow_ref, f, h) for f in range(20)]
-        for f in range(20):
-            store_part(base_ref, f, solve(diag_ref, f // 4, f % 4, flow))
+            untile(tables_ref, (1 + e) * 64, lambda lanes, e=e: diag_in[e, :, cells(lanes)], 5, 8, write_diag)
         for q in range(2):
             weight = [None] * 20
             for g in range(5):
@@ -280,11 +287,10 @@
             for e in range(5):
                 row = (e * 2 + q) * 8
                 map_ref[row : row + 8, :] = solve(diag_ref, e, 0, weight)
-        coupling = local_coupling(h, freq, src_ref, near_ref, jac_ref, beside_ref)
+        coupling = local_coupling(h, freq, src_ref, near_ref, jac_ref, beside_ref.at[h])
+        rest = [load_half(flow_ref, f, h) - coupling[f] for f in range(20)]
         for f in range(20):
-            store_part(part_ref, f, load_part(base_ref, f) - solve(diag_ref, f // 4, f % 4, coupling))
-
-    return body
+            store_part(part_ref, f, solve(diag_ref, f // 4, f % 4, rest))
 
 
 def wall_terms(freq, wall_of, map_ref):
@@ -298,17 +304,19 @@
     return terms
 
 
-def last_local(h):
-    def body(freq_ref, src_ref, near_ref, jac_ref, diag_ref, base_ref, map_ref, wall_ref, part_ref, beside_ref):
-        freq = own_freq(freq_ref)
+def last_kernel(freq_ref, src_ref, flow_ref, wall_ref, *refs):
+    freq = own_freq(freq_ref)
+    beside_ref = refs[10]
+    for h in range(2):
+        near_ref, jac_ref, diag_ref, map_ref = refs[h * 4 : h * 4 + 4]
+        part_ref = refs[8 + h]
         terms = wall_terms(freq, lambda v: wall_ref[v * 16 + h * 8 : v * 16 + h * 8 + 8, :], map_ref)
         for f in range(20):
-            store_part(part_ref, f, load_part(base_ref, f) + terms[f])
-        coupling = local_coupling(h, freq, src_ref, near_ref, jac_ref, beside_ref)
+            store_part(part_ref, f, terms[f])
+        coupling = local_coupling(h, freq, src_ref, near_ref, jac_ref, beside_ref.at[h])
+        rest = [load_half(flow_ref, f, h) - coupling[f] for f in range(20)]
         for f in range(20):
-            store_part(part_ref, f, load_part(part_ref, f) - solve(diag_ref, f // 4, f % 4, coupling))
-
-    return body
+            store_part(part_ref, f, load_part(part_ref, f) + solve(diag_ref, f // 4, f % 4, rest))
 
 
 def ghost_kernel(g0, g1, g2, g3, *refs):
@@ -362,7 +370,7 @@
 NEAR_FACE = (0,)
 NEAR_PICK = range(4)
 NEAR_SEND = (0,)
-ORDER = ((2, 2), (0, 1), (3, -2), (1, -1))
+ORDER = ((3, -2), (1, -1), (2, 2), (0, 1))
 
 
 def exchange(blocks):
@@ -391,9 +399,12 @@
     part, small, field = ((160, LANES), F32), ((80, LANES), F32), ((320, LANES), F32)
     dest = face_dest.reshape(32, LANES)
     coef = modal_coeff.transpose(1, 2, 0).reshape(16, 64)
-    faces = call(face_kernel, (coef, spline_blocks), [((4, 8, 1024), F32)], near_out=NEAR_FACE)[0]
+    operands = [pltpu.with_memory_space_constraint(x, pltpu.HBM) for x in (coef, spline_blocks)]
+    faces = call(face_kernel, operands, [((4, 8, 1024), F32)], near_out=NEAR_FACE)[0]
     faces = lax.all_to_all(faces, "rep", split_axis=0, concat_axis=0, tiled=True)
-    slot = call(slot_kernel, (dest,), [((32, LANES), jnp.int32)], near_out=(0,))[0]
+    slot, freq = call(
+        slot_kernel, (frequency, dest), [((32, LANES), jnp.int32), ((16, LANES), F32)], smem=1, near_out=(0, 1)
+    )
     prev = to_rows(previous)
     rows_out = send_list.reshape(8, LANES)
     picked = call(pick_kernel, (prev, rows_out), halo, near_out=NEAR_PICK)
@@ -408,30 +419,18 @@
     recv = lax.all_to_all(send.reshape(dom, 9, 1, LANES), "dom", split_axis=0, concat_axis=0, tiled=True)
     recv = recv.reshape(dom * 9, LANES)
 
-    half = neighbor.shape[1] // 2
     jac_in = off_jacobian.transpose(1, 2, 0, 3)
     flow, weight = to_rows(flow_rhs), to_rows(wall_weight)
-    beside = pltpu.VMEM((960, LANES), F32)
-    tables, parts, bases, maps = [], [], [], []
-    for h in range(2):
-        specs = {
-            2: pl.BlockSpec((6, half), lambda i, h=h: (0, h)),
-            3: pl.BlockSpec((5, 5, 6, half), lambda i, h=h: (0, 0, 0, h)),
-            4: pl.BlockSpec((5, 5, half), lambda i, h=h: (0, 0, h)),
-        }
-        near, jac, diag, p, b, m = call(
-            first_local(h),
-            (frequency, prev, neighbor, jac_in, diag_inverse, flow, weight),
-            [((48, LANES), jnp.int32), ((1200, LANES), F32), ((200, LANES), F32), part, part, small],
-            [pltpu.VMEM((31 * 64, LANES), F32), beside],
-            specs,
-            smem=1,
-            near_out=range(6),
-        )
-        tables += [(near,), (jac,), (diag,)]
-        parts.append((p,))
-        bases.append((b,))
-        maps.append((m,))
+    table = [((48, LANES), jnp.int32), ((1200, LANES), F32), ((200, LANES), F32), small, part]
+    made = call(
+        first_kernel,
+        ((freq,), prev, neighbor, jac_in, diag_inverse, flow, weight),
+        table * 2,
+        [pltpu.VMEM((2, 31 * 64, LANES), F32), pltpu.VMEM((2, 960, LANES), F32)],
+        near_out=range(10),
+    )
+    made = [(x,) for x in made]
+    tables, maps, parts = made[0:3] + made[5:8], [made[3], made[8]], [made[4], made[9]]
     both_beside = [pltpu.VMEM((2, 960, LANES), F32)]
 
     def ghost_part(ghosts, parts, near_out):
@@ -441,26 +440,20 @@
     pre = ghost_part(ghosts, parts, (0,))
     it, wall, *picked = call(
         wall_kernel,
-        (frequency, (recv,), (rows_out,), (pre,), *maps),
+        ((freq,), (recv,), (rows_out,), (pre,), *maps),
         [field, ((LANES, LANES), F32), *halo],
         [pltpu.VMEM((dom * 16, LANES), F32)],
-        smem=1,
         near_out=range(6),
     )
     ghosts = exchange(picked)
-    parts = []
-    for h in range(2):
-        parts.append(
-            call(
-                last_local(h),
-                (frequency, (it,), *tables[3 * h : 3 * h + 3], bases[h], maps[h], (wall,)),
-                [part],
-                [beside],
-                smem=1,
-                near_out=(0,),
-            )
-        )
-    out = ghost_part(ghosts, [tuple(p) for p in parts], ())
+    parts = call(
+        last_kernel,
+        ((freq,), (it,), flow, (wall,), *tables[:3], maps[0], *tables[3:], maps[1]),
+        [part, part],
+        both_beside,
+        near_out=(0, 1),
+    )
+    out = ghost_part(ghosts, [(p,) for p in parts], ())
     return from_rows(out, flow_rhs.shape)
 
 

time: 68.8 us -> 63.4 us (0.922)
  local copies, waits for them, and re-layouts: 3.57 us -> 0.05 us
  Pallas kernels: 22.6 us -> 21.3 us
    unnamed x32 -> x20, local copies, waits for them, and re-layouts: 3.56 us -> 0.04 us
    pallas_call x11 -> x9, Pallas kernels: 22.6 us -> 21.3 us  [call(): pl.pallas_call(body, grid=(1,), out_shape=shapes, in_specs=in_specs, out_...]
  transfers between devices with their start and end apart: 10 -> 10, of which waited for: 1 -> 1; matrix products, arithmetic and copies ran while one was open for 0% -> 0% of each run, Pallas kernels for 21% -> 20%
where the time goes in v4:
time: 63.4 us; the launch traced here: 63.1 us
  starting transfers between devices  38.1 us (60%)
  Pallas kernels  21.3 us (34%)
  waiting for transfers between devices  3.5 us (6%)
    pallas_call x9, Pallas kernels, call(): pl.pallas_call(body, grid=(1,), out_shape=shapes, in_specs=in_specs, out_...  21.3 us
    ppermute x8, starting transfers between devices, from_behind(): lax.ppermute(value, axis, [(i, (i + by) % length) for i in range(length)])  21 us
    all_to_all x1, starting transfers between devices, step(): lax.all_to_all(send.reshape(dom, 9, 1, LANES), 'dom', split_axis=0, conca...  11.5 us
    all_to_all x1, starting transfers between devices, step(): lax.all_to_all(faces, 'rep', split_axis=0, concat_axis=0, tiled=True)  5.56 us
    all_to_all x1, waiting for transfers between devices, step(): lax.all_to_all(faces, 'rep', split_axis=0, concat_axis=0, tiled=True)  3.48 us
  transfers between devices with their start and end apart: 10, of which 1 were waited for; matrix products, arithmetic and copies ran while one was open for 0% of the time, Pallas kernels for 20%

profile of v4, /device:TPU:8, one launch (start us, length us, event | category | flops | bytes accessed | tf_op | source)
XLA Modules:
  0.0 63.1 jit_solution(4625180753667184404)
XLA Ops:
  0.0 0.0 copy-start.6
  0.0 0.0 copy-start.8
  0.0 0.0 copy-start.7
  0.0 0.0 copy-start.4
  0.0 1.9 %shard_map.119 = f32[4,8,1024]{2,1,0:T(8,128)} custom-call(bf16[16,64]{1,0:T(8,128)(2,1)} %bitcast.38, bf16[8,2,64,128]{3,2,1,0:T(8,128)(2,1)} %spline_ref.1), custom_call_target="tpu_custom_call" | custom-call | tf_op jit(solution)/shard_map/pallas_call | solution.py:39
  1.9 0.0 copy-start
  1.9 5.6 %all-to-all-start = ((f32[4,8,1024]{2,1,0:T(8,128)}), f32[4,8,1024]{2,1,0:T(8,128)S(1)}, u32[]{:S(2)}, u32[]{:S(2)}) async-start(f32[4,8,1024]{2,1,0:T(8,128)} %shard_map.119), calls=%async_computation | async-start | bytes 262144 | tf_op jit(solution)/shard_map/all_to_all | solution.py:404
  7.4 0.0 copy-done.6
  7.5 0.0 copy-done.8
  7.5 1.0 %shard_map.118 = (s32[32,128]{1,0:T(8,128)S(1)}, f32[16,128]{1,0:T(8,128)S(1)}) custom-call(f32[8]{0:T(128)S(1)} %copy-done.8, s32[32,128]{1,0:T(8,128)S(1)} %bitcast.35), custom_call_target="tpu_custom_call" | custom-call | tf_op jit(solution)/shard_map/pallas_call | solution.py:39
  8.5 3.5 %all-to-all-done.vals_ref = f32[4,8,1024]{2,1,0:T(8,128)S(1)} async-done(((f32[4,8,1024]{2,1,0:T(8,128)}), f32[4,8,1024]{2,1,0:T(8,128)S(1)}, u32[]{:S(2)}, u32[]{:S(2)}) %all-to-all-start) | async-done | bytes 131104 | tf_op jit(solution)/shard_map/all_to_all | solution.py:404
  12.0 0.0 copy-done.7
  12.0 0.0 copy-start.9
  12.0 2.1 %shard_map.120 = f32[576,128]{1,0:T(8,128)} custom-call(f32[4,8,1024]{2,1,0:T(8,128)S(1)} %all-to-all-done.vals_ref, s32[32,128]{1,0:T(8,128)S(1)} %bitcast.36, s32[32,128]{1,0:T(8,128)S(1)} %get-tuple-element.30.slot_ref, s32[32,128]{1,0:T(8,128)S(1)} %bitcast.37), custom_call_target="tpu_custom_call" | custom-call | tf_op jit(solution)/shard_map/pallas_call | solution.py:39
  14.1 0.0 copy-start.1
  14.1 0.0 copy-start.3
  14.1 0.0 copy-start.5
  14.1 11.5 %all-to-all-start.1 = ((f32[64,9,1,128]{3,2,1,0:T(1,128)}), f32[64,9,1,128]{3,2,1,0:T(1,128)S(1)}, u32[]{:S(2)}, u32[]{:S(2)}) async-start(f32[64,9,1,128]{3,2,1,0:T(1,128)} %bitcast.4), calls=%async_computation.1 | async-start | bytes 589824 | tf_op jit(solution)/shard_map/all_to_all | solution.py:419
  25.7 0.0 copy-done.9
  25.7 0.0 copy-start.2
  25.7 0.0 copy-done.1
  25.7 0.4 shard_map.121
  26.1 0.1 collective-permute-start
  26.3 5.0 %collective-permute-start.1 = (f32[40,128]{1,0:T(8,128)S(1)}, f32[40,128]{1,0:T(8,128)S(1)}, u32[]{:S(2)}, u32[]{:S(2)}) collective-permute-start(f32[40,128]{1,0:T(8,128)S(1)} %get-tuple-element.32), channel_id=1, source_target_pairs={{0,252},{4,0},{8,4},{12,8},{16,12},{20,16},{24,20},{28,24},{32,28}... | collective-permute-start | bytes 61448 | tf_op jit(solution)/shard_map/ppermute | solution.py:16
  31.3 0.0 collective-permute-start.2
  31.3 5.3 %collective-permute-start.3 = (f32[40,128]{1,0:T(8,128)S(1)}, f32[40,128]{1,0:T(8,128)S(1)}, u32[]{:S(2)}, u32[]{:S(2)}) collective-permute-start(f32[40,128]{1,0:T(8,128)S(1)} %get-tuple-element.34), channel_id=1, source_target_pairs={{0,248},{4,252},{8,0},{12,4},{16,8},{20,12},{24,16},{28,20},{32,24... | collective-permute-start | bytes 61448 | tf_op jit(solution)/shard_map/ppermute | solution.py:16
  36.6 0.0 copy-done.4
  36.6 0.0 copy-done
  36.6 0.0 copy-done.3
  36.6 0.0 copy-done.5
  36.6 0.0 copy-done.2
  36.6 4.7 %shard_map.122 = (s32[48,128]{1,0:T(8,128)S(1)}, f32[1200,128]{1,0:T(8,128)S(1)}, f32[200,128]{1,0:T(8,128)S(1)}, f32[80,128]{1,0:T(8,128)S(1)}, f32[160,128]{1,...) custom-call(f32[16,128]{1,0:T(8,128)S(1)} %get-tuple-element.29.freq, ...), custom_call_target="tpu_custom_call" | custom-call | tf_op jit(solution)/shard_map/pallas_call | solution.py:39
  41.3 0.0 collective-permute-done.g0
  41.3 0.0 collective-permute-done.1.g1
  41.3 0.0 collective-permute-done.2.g2
  41.3 0.0 collective-permute-done.3.g3
  41.4 2.3 %shard_map.123.pre_ref = f32[320,128]{1,0:T(8,128)S(1)} custom-call(f32[40,128]{1,0:T(8,128)S(1)} %collective-permute-done.g0, f32[40,128]{1,0:T(8,128)S(1)} %collective-permute-done.1.g1, f32[40,128]{1,0:T(8,128)S(1)} %collective-permute-done.2.g2, f32[40,128]{1,0:T(8,128)S(1)} %collective-permute-done.3.g3, s32[48,128]{1,0:T(8,128)S(1)} %get-tuple-element.35.refs_0_, ...), custom_call_target="tpu_custom_call" | custom-call | tf_op jit(solution)/shard_map/pallas_call | solution.py:39
  43.6 0.0 all-to-all-done.1
  43.6 1.7 %shard_map.124 = (f32[320,128]{1,0:T(8,128)S(1)}, f32[128,128]{1,0:T(8,128)S(1)}, f32[40,128]{1,0:T(8,128)S(1)}, f32[40,128]{1,0:T(8,128)S(1)}, f32[40,128]{1,0:T(8,128)S(1)}, /*index=5*/f32[40,128]{1,0:T(8,128)S(1)}) custom-call(f32[16,128]{1,0:T(8,128)S(1)} %get-tuple-element.29.freq_ref, f32[576,128]{1,0:T(8,128)S(1)} %bitcast.28, ...), custom_call_target="tpu_custom_call" | custom-call | tf_op jit(solution)/shard_map/pallas_call | solution.py:39
  45.3 0.1 collective-permute-start.4
  45.4 5.1 %collective-permute-start.5 = (f32[40,128]{1,0:T(8,128)S(1)}, f32[40,128]{1,0:T(8,128)S(1)}, u32[]{:S(2)}, u32[]{:S(2)}) collective-permute-start(f32[40,128]{1,0:T(8,128)S(1)} %get-tuple-element.46), channel_id=1, source_target_pairs={{0,252},{4,0},{8,4},{12,8},{16,12},{20,16},{24,20},{28,24},{32,28}... | collective-permute-start | bytes 61448 | tf_op jit(solution)/shard_map/ppermute | solution.py:16
  50.4 0.0 collective-permute-start.6
  50.4 5.3 %collective-permute-start.7 = (f32[40,128]{1,0:T(8,128)S(1)}, f32[40,128]{1,0:T(8,128)S(1)}, u32[]{:S(2)}, u32[]{:S(2)}) collective-permute-start(f32[40,128]{1,0:T(8,128)S(1)} %get-tuple-element.48), channel_id=1, source_target_pairs={{0,248},{4,252},{8,0},{12,4},{16,8},{20,12},{24,16},{28,20},{32,24... | collective-permute-start | bytes 61448 | tf_op jit(solution)/shard_map/ppermute | solution.py:16
  55.8 4.3 %shard_map.125 = (f32[160,128]{1,0:T(8,128)S(1)}, f32[160,128]{1,0:T(8,128)S(1)}) custom-call(f32[16,128]{1,0:T(8,128)S(1)} %get-tuple-element.29.freq_ref, f32[320,128]{1,0:T(8,128)S(1)} %get-tuple-element.49.src_ref, f32[320,128]{1,0:T(8,128)S(1)} %bitcast.33, f32[128,128]{1,0:T(8,128)S(1)} %get-tuple-element.50.wall_ref, ...), custom_call_target="tpu_custom_call" | custom-call | tf_op jit(solution)/shard_map/pallas_call | solution.py:39
  60.1 0.0 collective-permute-done.4.g0
  60.1 0.0 collective-permute-done.5.g1
  60.1 0.0 collective-permute-done.6.g2
  60.2 0.0 collective-permute-done.7.g3
  60.2 3.0 %shard_map.126 = f32[320,128]{1,0:T(8,128)} custom-call(f32[40,128]{1,0:T(8,128)S(1)} %collective-permute-done.4.g0, f32[40,128]{1,0:T(8,128)S(1)} %collective-permute-done.5.g1, f32[40,128]{1,0:T(8,128)S(1)} %collective-permute-done.6.g2, f32[40,128]{1,0:T(8,128)S(1)} %collective-permute-done.7.g3, s32[48,128]{1,0:T(8,128)S(1)} %get-tuple-element.35.refs_0_, ...), custom_call_target="tpu_custom_call" | custom-call | tf_op jit(solution)/shard_map/pallas_call | solution.py:39
  (1 shorter events, 0.0 us)
Async XLA Ops:
  0.0 7.5 %copy-start.6 = (s32[4096,1]{0,1:T(1,128)S(1)}, s32[4096,1]{0,1:T(1,128)}, u32[]{:S(2)}) copy-start(s32[4096,1]{0,1:T(1,128)} %param.15) | copy-start | bytes 49156
  0.0 7.5 %copy-start.8 = (f32[8]{0:T(128)S(1)}, f32[8]{0:T(128)}, u32[]{:S(2)}) copy-start(f32[8]{0:T(128)} %freq_ref.1) | copy-start | bytes 100
  0.0 12.0 %copy-start.7 = (s32[4096]{0:T(1024)S(1)}, s32[4096]{0:T(1024)}, u32[]{:S(2)}) copy-start(s32[4096]{0:T(1024)} %param.16) | copy-start | bytes 49156
  0.0 36.6 %copy-start.4 = (f32[5,2,2048]{2,1,0:T(2,128)S(1)}, f32[5,2,2048]{2,1,0:T(2,128)}, u32[]{:S(2)}) copy-start(f32[5,2,2048]{2,1,0:T(2,128)} %param.17) | copy-start | bytes 245764
  1.9 34.7 %copy-start = (bf16[6,5,5,2048]{3,0,2,1:T(8,128)(2,1)S(1)}, bf16[6,5,5,2048]{3,0,2,1:T(8,128)(2,1)}, u32[]{:S(2)}) copy-start(bf16[6,5,5,2048]{3,0,2,1:T(8,128)(2,1)} %param.21) | copy-start | bytes 1843204
  1.9 10.1 %all-to-all-start = ((f32[4,8,1024]{2,1,0:T(8,128)}), f32[4,8,1024]{2,1,0:T(8,128)S(1)}, u32[]{:S(2)}, u32[]{:S(2)}) async-start(f32[4,8,1024]{2,1,0:T(8,128)} %shard_map.119), calls=%async_computation | async-start | bytes 262144 | tf_op jit(solution)/shard_map/all_to_all | solution.py:404
  12.0 13.7 %copy-start.9 = (s32[4,256]{1,0:T(4,128)S(1)}, s32[4,256]{1,0:T(4,128)}, u32[]{:S(2)}) copy-start(s32[4,256]{1,0:T(4,128)} %param.23) | copy-start | bytes 12292
  14.1 11.6 %copy-start.1 = (f32[5,2,2,2048]{3,2,1,0:T(2,128)S(1)}, f32[5,2,2,2048]{3,2,1,0:T(2,128)}, u32[]{:S(2)}) copy-start(f32[5,2,2,2048]{3,2,1,0:T(2,128)} %param.19) | copy-start | bytes 491524
  14.1 22.5 %copy-start.3 = (f32[5,5,2048]{2,1,0:T(8,128)S(1)}, f32[5,5,2048]{2,1,0:T(8,128)}, u32[]{:S(2)}) copy-start(f32[5,5,2048]{2,1,0:T(8,128)} %diag_in.1) | copy-start | bytes 614404
  14.1 22.5 %copy-start.5 = (s32[6,2048]{1,0:T(8,128)S(1)}, s32[6,2048]{1,0:T(8,128)}, u32[]{:S(2)}) copy-start(s32[6,2048]{1,0:T(8,128)} %near_in.1) | copy-start | bytes 147460
  14.1 29.5 %all-to-all-start.1 = ((f32[64,9,1,128]{3,2,1,0:T(1,128)}), f32[64,9,1,128]{3,2,1,0:T(1,128)S(1)}, u32[]{:S(2)}, u32[]{:S(2)}) async-start(f32[64,9,1,128]{3,2,1,0:T(1,128)} %bitcast.4), calls=%async_computation.1 | async-start | bytes 589824 | tf_op jit(solution)/shard_map/all_to_all | solution.py:419
  25.7 11.0 %copy-start.2 = (f32[5,2,2,2048]{3,2,1,0:T(2,128)S(1)}, f32[5,2,2,2048]{3,2,1,0:T(2,128)}, u32[]{:S(2)}) copy-start(f32[5,2,2,2048]{3,2,1,0:T(2,128)} %param.18) | copy-start | bytes 491524
  26.1 15.2 %collective-permute-start = (f32[40,128]{1,0:T(8,128)S(1)}, f32[40,128]{1,0:T(8,128)S(1)}, u32[]{:S(2)}, u32[]{:S(2)}) collective-permute-start(f32[40,128]{1,0:T(8,128)S(1)} %get-tuple-element.31), channel_id=1, source_target_pairs={{0,4},{4,8},{8,12},{12,16},{16,20},{20,24},{24,28},{28,32},{32,36}... | collective-permute-start | bytes 61448 | tf_op jit(solution)/shard_map/ppermute | solution.py:16
  26.3 15.1 %collective-permute-start.1 = (f32[40,128]{1,0:T(8,128)S(1)}, f32[40,128]{1,0:T(8,128)S(1)}, u32[]{:S(2)}, u32[]{:S(2)}) collective-permute-start(f32[40,128]{1,0:T(8,128)S(1)} %get-tuple-element.32), channel_id=1, source_target_pairs={{0,252},{4,0},{8,4},{12,8},{16,12},{20,16},{24,20},{28,24},{32,28}... | collective-permute-start | bytes 61448 | tf_op jit(solution)/shard_map/ppermute | solution.py:16
  31.3 10.1 %collective-permute-start.2 = (f32[40,128]{1,0:T(8,128)S(1)}, f32[40,128]{1,0:T(8,128)S(1)}, u32[]{:S(2)}, u32[]{:S(2)}) collective-permute-start(f32[40,128]{1,0:T(8,128)S(1)} %get-tuple-element.33), channel_id=1, source_target_pairs={{0,8},{4,12},{8,16},{12,20},{16,24},{20,28},{24,32},{28,36},{32,40... | collective-permute-start | bytes 61448 | tf_op jit(solution)/shard_map/ppermute | solution.py:16
  31.3 10.1 %collective-permute-start.3 = (f32[40,128]{1,0:T(8,128)S(1)}, f32[40,128]{1,0:T(8,128)S(1)}, u32[]{:S(2)}, u32[]{:S(2)}) collective-permute-start(f32[40,128]{1,0:T(8,128)S(1)} %get-tuple-element.34), channel_id=1, source_target_pairs={{0,248},{4,252},{8,0},{12,4},{16,8},{20,12},{24,16},{28,20},{32,24... | collective-permute-start | bytes 61448 | tf_op jit(solution)/shard_map/ppermute | solution.py:16
  45.3 14.8 %collective-permute-start.4 = (f32[40,128]{1,0:T(8,128)S(1)}, f32[40,128]{1,0:T(8,128)S(1)}, u32[]{:S(2)}, u32[]{:S(2)}) collective-permute-start(f32[40,128]{1,0:T(8,128)S(1)} %get-tuple-element.45), channel_id=1, source_target_pairs={{0,4},{4,8},{8,12},{12,16},{16,20},{20,24},{24,28},{28,32},{32,36}... | collective-permute-start | bytes 61448 | tf_op jit(solution)/shard_map/ppermute | solution.py:16
  45.4 14.7 %collective-permute-start.5 = (f32[40,128]{1,0:T(8,128)S(1)}, f32[40,128]{1,0:T(8,128)S(1)}, u32[]{:S(2)}, u32[]{:S(2)}) collective-permute-start(f32[40,128]{1,0:T(8,128)S(1)} %get-tuple-element.46), channel_id=1, source_target_pairs={{0,252},{4,0},{8,4},{12,8},{16,12},{20,16},{24,20},{28,24},{32,28}... | collective-permute-start | bytes 61448 | tf_op jit(solution)/shard_map/ppermute | solution.py:16
  50.4 9.7 %collective-permute-start.6 = (f32[40,128]{1,0:T(8,128)S(1)}, f32[40,128]{1,0:T(8,128)S(1)}, u32[]{:S(2)}, u32[]{:S(2)}) collective-permute-start(f32[40,128]{1,0:T(8,128)S(1)} %get-tuple-element.47), channel_id=1, source_target_pairs={{0,8},{4,12},{8,16},{12,20},{16,24},{20,28},{24,32},{28,36},{32,40... | collective-permute-start | bytes 61448 | tf_op jit(solution)/shard_map/ppermute | solution.py:16
  50.4 9.7 %collective-permute-start.7 = (f32[40,128]{1,0:T(8,128)S(1)}, f32[40,128]{1,0:T(8,128)S(1)}, u32[]{:S(2)}, u32[]{:S(2)}) collective-permute-start(f32[40,128]{1,0:T(8,128)S(1)} %get-tuple-element.48), channel_id=1, source_target_pairs={{0,248},{4,252},{8,0},{12,4},{16,8},{20,12},{24,16},{28,20},{32,24... | collective-permute-start | bytes 61448 | tf_op jit(solution)/shard_map/ppermute | solution.py:16
